TPU v7x, 32 devices: a whole 2x2x4 slice. The times are simulated.
32 devices in a mesh: space: 2 (over y), inner: 16 (over z, x, core).
Axes of the slice: x: 2, y: 2, z: 4, core: 2. Of those that a mesh axis runs over, the one named last changes fastest.
Arguments:
- hamiltonian: bfloat16 [64, 5, 128, 128], P(('space', 'inner')), as said below
- pattern: int32 [64, 5], P(('space', 'inner')), may hold values from 0 to 1, as said below
- ortho: bfloat16 [64, 2, 128, 128], P(('space', 'inner')), may hold values from -0.25 to 0.25
- lists: int32 [64, 6], P(('space', 'inner')), may hold values from -1 to 63, as said below
Outputs:
- density: float32 [64, 13, 128, 128], P(('space', 'inner'))
Inputs may be any that keep to these rules, and one draw needn't show every extreme that they name: Symmetric block band: hamiltonian[j, r] is the transpose of hamiltonian[j + r - 2, 4 - r]; blocks that point outside the matrix are zero. symmetric: pattern[j, r] equals pattern[j + r - 2, 4 - r]; the middle entry is 1; entries that point outside the matrix are 0. lists[j, 0] = j; the next entries are distinct block columns within 5 of j other than j, followed only by -1; each row has 3 to 6 entries that are not -1, and some row has 6.
All inputs are finite; a program needn't handle non-finite values.
Results may differ from a plain program's by a relative error of at most 0.0055.
Values may be sent and summed in bfloat16 or wider, within the bound.
A program may use at most 64 MiB of HBM per device.

v0:
```python
import jax
import jax.numpy as jnp
import numpy as np
from jax import lax
from jax.sharding import PartitionSpec as P

RO = 3
Q = 5
STEPS = 3


chem_level = 0.25


def shifted_2(value, axis, by):
    length = lax.axis_size(axis)
    pairs = [(i, i + by) for i in range(length) if 0 <= i + by < length]
    return lax.ppermute(value, axis, pairs)


def orth_columns(ham_ext, ortho_ext, ham_off, ortho_off, count, first_row):
    column_range = np.arange(count)
    previous = ham_ext[ham_off + column_range - 1]
    current = ham_ext[ham_off + column_range]
    upper = ortho_ext[ortho_off + column_range, 0]
    diagonal = ortho_ext[ortho_off + column_range, 1]
    row_index = ortho_off + column_range[:, None] + np.arange(first_row - RO, RO + 1)[None, :]
    z_rows = ortho_ext[row_index]
    left_padded = jnp.pad(previous, ((0, 0), (1, 2), (0, 0), (0, 0)))[:, first_row:]
    right_padded = jnp.pad(current, ((0, 0), (2, 1), (0, 0), (0, 0)))[:, first_row:]
    product = jnp.einsum("cgab,cbd->cgad", left_padded, upper, preferred_element_type=jnp.float32)
    product = product + jnp.einsum(
        "cgab,cbd->cgad", right_padded, diagonal, preferred_element_type=jnp.float32
    )
    product = product.astype(jnp.bfloat16)
    result = jnp.einsum(
        "cqba,cqbd->cqad", z_rows[:, :, 0], product[:, :-1], preferred_element_type=jnp.float32
    )
    result = result + jnp.einsum(
        "cqba,cqbd->cqad", z_rows[:, :, 1], product[:, 1:], preferred_element_type=jnp.float32
    )
    return result.astype(jnp.bfloat16)


def mat_product(left, right):
    return jnp.dot(left, right, preferred_element_type=jnp.float32)


def solve_column(orth_ext, base, slots, column):
    positions = jnp.clip(slots - base, 0, orth_ext.shape[0] - 1).astype(jnp.int32)
    gathered = orth_ext[positions]
    first_row = 2 * RO + 1 - gathered.shape[1]
    live = slots >= 0
    both_live = live[:, None, None] & live[None, :, None]
    offsets_grid = slots[:, None] - slots[None, :] + RO
    band_rows = jnp.arange(first_row, 2 * RO + 1, dtype=jnp.int32)[None, None, :]
    lower_sel = (
        (offsets_grid[:, :, None] == band_rows) & (offsets_grid >= RO)[:, :, None] & both_live
    )
    upper_sel = (
        ((2 * RO - offsets_grid)[:, :, None] == band_rows)
        & (offsets_grid < RO)[:, :, None]
        & both_live
    )
    sub_block = jnp.einsum(
        "str,trab->satb",
        lower_sel.astype(jnp.bfloat16),
        gathered,
        preferred_element_type=jnp.float32,
    )
    sub_block = sub_block + jnp.einsum(
        "str,srba->satb",
        upper_sel.astype(jnp.bfloat16),
        gathered,
        preferred_element_type=jnp.float32,
    )
    slot_count = gathered.shape[0]
    block_size = gathered.shape[-1]
    order_n = slot_count * block_size
    sub_block = sub_block.reshape(order_n, order_n)
    diag_values = jnp.repeat(live.astype(jnp.float32), block_size)
    shifted = chem_level * jnp.diag(diag_values) - sub_block
    squares = jnp.sum(shifted * shifted)
    live_rows = jnp.sum(live.astype(jnp.float32)) * block_size
    scale = 2.0 * jnp.sqrt(squares / live_rows + 1e-06)
    iterate = (shifted / scale).astype(jnp.bfloat16)
    identity = jnp.eye(order_n, dtype=jnp.float32)
    for step_index in range(STEPS - 1):
        square = mat_product(iterate, iterate)
        factor = (1.5 * identity - 0.5 * square).astype(jnp.bfloat16)
        iterate = mat_product(iterate, factor).astype(jnp.bfloat16)
    columns = iterate[:, :block_size]
    unit = identity[:, :block_size]
    square_col = mat_product(iterate, columns)
    factor_col = (1.5 * unit - 0.5 * square_col).astype(jnp.bfloat16)
    result = mat_product(iterate, factor_col)
    pcol = (0.5 * (unit + result)).reshape(slot_count, block_size, block_size)
    placing = (
        ((slots - column + Q)[:, None] == jnp.arange(2 * Q + 1, dtype=jnp.int32)[None, :])
        & live[:, None]
    ).astype(jnp.float32)
    return jnp.einsum("sr,sab->rab", placing, pcol, precision=lax.Precision.HIGHEST)


def back_transform(porth, porth_next, ortho_ext, ortho_off, count):
    column_range = np.arange(count)
    diag_own = ortho_ext[ortho_off + column_range, 1].astype(jnp.float32)
    upper_next = ortho_ext[ortho_off + column_range + 1, 0].astype(jnp.float32)
    low_band = jnp.pad(porth, ((0, 0), (0, 1), (0, 0), (0, 0)))
    high_band = jnp.pad(porth_next, ((0, 0), (1, 0), (0, 0), (0, 0)))
    right_part = jnp.einsum("crab,cdb->crad", low_band, diag_own, precision=lax.Precision.HIGHEST)
    right_part = right_part + jnp.einsum(
        "crab,cdb->crad", high_band, upper_next, precision=lax.Precision.HIGHEST
    )
    row_index = ortho_off + column_range[:, None] + np.arange(-Q - 1, Q + 2)[None, :]
    diag_rows = ortho_ext[row_index, 1].astype(jnp.float32)
    upper_rows = ortho_ext[row_index + 1, 0].astype(jnp.float32)
    lower_y = jnp.pad(right_part, ((0, 0), (1, 0), (0, 0), (0, 0)))
    upper_y = jnp.pad(right_part, ((0, 0), (0, 1), (0, 0), (0, 0)))
    result = jnp.einsum("cpab,cpbd->cpad", diag_rows, lower_y, precision=lax.Precision.HIGHEST)
    return result + jnp.einsum(
        "cpab,cpbd->cpad", upper_rows, upper_y, precision=lax.Precision.HIGHEST
    )


def local(hamiltonian, pattern, ortho, lists):
    local_count = hamiltonian.shape[0]
    block_size = hamiltonian.shape[-1]
    first = lax.axis_index(("space", "inner")) * local_count
    masked = hamiltonian * pattern[:, :, None, None].astype(jnp.bfloat16)
    global_cols = first + jnp.arange(local_count, dtype=jnp.int32)
    upper = jnp.where((global_cols == 0)[:, None, None], jnp.zeros_like(ortho[:, 0]), ortho[:, 0])
    diag_z = (jnp.eye(block_size, dtype=jnp.float32) + ortho[:, 1].astype(jnp.float32)).astype(
        jnp.bfloat16
    )
    stacked = jnp.stack([upper, diag_z], 1)
    ham_reach = -(-Q // local_count)
    ortho_reach = -(-(Q + 2) // local_count)
    ortho_pieces = []
    for offset in range(-ortho_reach, ortho_reach + 1):
        if offset == 0:
            ortho_pieces.append(stacked)
        else:
            ortho_pieces.append(shifted_2(stacked, ("space", "inner"), -offset))
    ortho_ext = jnp.concatenate(ortho_pieces, 0)
    left_piece = shifted_2(masked[-1:], ("space", "inner"), 1)
    with_left = jnp.concatenate([left_piece, masked], 0)
    strip_pieces = []
    own_orth = orth_columns(with_left, ortho_ext, 1, ortho_reach * local_count, local_count, RO)
    for offset in range(-ham_reach, ham_reach + 1):
        if offset == 0:
            strip_pieces.append(own_orth)
        else:
            strip_pieces.append(shifted_2(own_orth, ("space", "inner"), -offset))
    orth_ext = jnp.concatenate(strip_pieces, 0)
    orth_base = first - ham_reach * local_count
    bands = lax.map(
        lambda item: solve_column(orth_ext, orth_base, item[0], item[1]), (lists, global_cols)
    )
    next_piece = shifted_2(bands[:1].astype(jnp.bfloat16), ("space", "inner"), -1).astype(
        jnp.float32
    )
    following = jnp.concatenate([bands[1:], next_piece], 0)
    return back_transform(bands, following, ortho_ext, ortho_reach * local_count, local_count)


def solution(mesh):
    in_specs = (
        P(("space", "inner"), None, None, None),
        P(("space", "inner"), None),
        P(("space", "inner"), None, None, None),
        P(("space", "inner"), None),
    )
    out_specs = P(("space", "inner"), None, None, None)
    return jax.shard_map(local, mesh=mesh, in_specs=in_specs, out_specs=out_specs, check_vma=False)
```

profile of v0, /device:TPU:1, one launch (start us, length us, event | category | flops | bytes accessed | tf_op | source)
XLA Modules:
  0.0 161.5 jit_solution(5997737061731994768)
XLA Ops:
  1.8 4.0 %collective-permute-start = (bf16[2,2,128,128]{3,2,1,0:T(8,128)(2,1)S(1)}, bf16[2,2,128,128]{3,2,1,0:T(8,128)(2,1)S(1)}, u32[]{:S(2)}, u32[]{:S(2)}) collective-permute-start(bf16[2,2,128,128]{3,2,1,0:T(8,128)(2,1)S(1)} %pad_maximum_fusion.1), channel_id=1, source_target_pairs={{0,4},{1,5},{2,6},{3,7},{4,8},{5,9},{6,10},{7,11},{8,12},{9,13},{1... | collective-permute-start | bytes 393224 | tf_op jit(solution)/shard_map/ppermute | solution.py:18
  5.9 4.0 %collective-permute-start.1 = (bf16[2,2,128,128]{3,2,1,0:T(8,128)(2,1)S(1)}, bf16[2,2,128,128]{3,2,1,0:T(8,128)(2,1)S(1)}, u32[]{:S(2)}, u32[]{:S(2)}) collective-permute-start(bf16[2,2,128,128]{3,2,1,0:T(8,128)(2,1)S(1)} %pad_maximum_fusion.1), channel_id=1, source_target_pairs={{0,3},{1,4},{2,5},{3,6},{4,7},{5,8},{6,9},{7,10},{8,11},{9,12},{10... | collective-permute-start | bytes 393224 | tf_op jit(solution)/shard_map/ppermute | solution.py:18
  9.9 3.1 %collective-permute-start.2 = (bf16[2,2,128,128]{3,2,1,0:T(8,128)(2,1)S(1)}, bf16[2,2,128,128]{3,2,1,0:T(8,128)(2,1)S(1)}, u32[]{:S(2)}, u32[]{:S(2)}) collective-permute-start(bf16[2,2,128,128]{3,2,1,0:T(8,128)(2,1)S(1)} %pad_maximum_fusion.1), channel_id=1, source_target_pairs={{0,2},{1,3},{2,4},{3,5},{4,6},{5,7},{6,8},{7,9},{8,10},{9,11},{10,... | collective-permute-start | bytes 393224 | tf_op jit(solution)/shard_map/ppermute | solution.py:18
  13.1 2.8 %collective-permute-start.3 = (bf16[2,2,128,128]{3,2,1,0:T(8,128)(2,1)S(1)}, bf16[2,2,128,128]{3,2,1,0:T(8,128)(2,1)S(1)}, u32[]{:S(2)}, u32[]{:S(2)}) collective-permute-start(bf16[2,2,128,128]{3,2,1,0:T(8,128)(2,1)S(1)} %pad_maximum_fusion.1), channel_id=1, source_target_pairs={{0,1},{1,2},{2,3},{3,4},{4,5},{5,6},{6,7},{7,8},{8,9},{9,10},{10,1... | collective-permute-start | bytes 393224 | tf_op jit(solution)/shard_map/ppermute | solution.py:18
  24.9 4.3 %collective-permute-start.8 = (bf16[1,5,128,128]{3,2,1,0:T(8,128)(2,1)S(1)}, bf16[1,5,128,128]{3,2,1,0:T(8,128)(2,1)S(1)}, u32[]{:S(2)}, u32[]{:S(2)}) collective-permute-start(bf16[1,5,128,128]{3,2,1,0:T(8,128)(2,1)S(1)} %slice.77), channel_id=1, source_target_pairs={{0,1},{1,2},{2,3},{3,4},{4,5},{5,6},{6,7},{7,8},{8,9},{9,10},{10,1... | collective-permute-start | bytes 491528 | tf_op jit(solution)/shard_map/ppermute | solution.py:18
  29.3 2.9 %collective-permute-done.6 = bf16[2,2,128,128]{3,2,1,0:T(8,128)(2,1)S(1)} collective-permute-done((bf16[2,2,128,128]{3,2,1,0:T(8,128)(2,1)S(1)}, bf16[2,2,128,128]{3,2,1,0:T(8,128)(2,1)S(1)}, u32[]{:S(2)}, u32[]{:S(2)}) %collective-permute-start.6) | collective-permute-done | bytes 131104 | tf_op jit(solution)/shard_map/ppermute | solution.py:18
  32.3 2.3 %collective-permute-done.7 = bf16[2,2,128,128]{3,2,1,0:T(8,128)(2,1)S(1)} collective-permute-done((bf16[2,2,128,128]{3,2,1,0:T(8,128)(2,1)S(1)}, bf16[2,2,128,128]{3,2,1,0:T(8,128)(2,1)S(1)}, u32[]{:S(2)}, u32[]{:S(2)}) %collective-permute-start.7) | collective-permute-done | bytes 131104 | tf_op jit(solution)/shard_map/ppermute | solution.py:18
  38.9 3.7 %collective-permute-start.9 = (bf16[2,4,128,128]{3,2,1,0:T(8,128)(2,1)S(1)}, bf16[2,4,128,128]{3,2,1,0:T(8,128)(2,1)S(1)}, u32[]{:S(2)}, u32[]{:S(2)}) collective-permute-start(bf16[2,4,128,128]{3,2,1,0:T(8,128)(2,1)S(1)} %fusion.64), channel_id=1, source_target_pairs={{0,3},{1,4},{2,5},{3,6},{4,7},{5,8},{6,9},{7,10},{8,11},{9,12},{10... | collective-permute-start | bytes 786440 | tf_op jit(solution)/shard_map/ppermute | solution.py:18
  42.6 2.8 %collective-permute-start.10 = (bf16[2,4,128,128]{3,2,1,0:T(8,128)(2,1)S(1)}, bf16[2,4,128,128]{3,2,1,0:T(8,128)(2,1)S(1)}, u32[]{:S(2)}, u32[]{:S(2)}) collective-permute-start(bf16[2,4,128,128]{3,2,1,0:T(8,128)(2,1)S(1)} %fusion.64), channel_id=1, source_target_pairs={{0,2},{1,3},{2,4},{3,5},{4,6},{5,7},{6,8},{7,9},{8,10},{9,11},{10,... | collective-permute-start | bytes 786440 | tf_op jit(solution)/shard_map/ppermute | solution.py:18
  45.4 3.0 %collective-permute-start.11 = (bf16[2,4,128,128]{3,2,1,0:T(8,128)(2,1)S(1)}, bf16[2,4,128,128]{3,2,1,0:T(8,128)(2,1)S(1)}, u32[]{:S(2)}, u32[]{:S(2)}) collective-permute-start(bf16[2,4,128,128]{3,2,1,0:T(8,128)(2,1)S(1)} %fusion.64), channel_id=1, source_target_pairs={{0,1},{1,2},{2,3},{3,4},{4,5},{5,6},{6,7},{7,8},{8,9},{9,10},{10,1... | collective-permute-start | bytes 786440 | tf_op jit(solution)/shard_map/ppermute | solution.py:18
  56.1 11.6 %collective-permute-done.12 = bf16[2,4,128,128]{3,2,1,0:T(8,128)(2,1)S(1)} collective-permute-done((bf16[2,4,128,128]{3,2,1,0:T(8,128)(2,1)S(1)}, bf16[2,4,128,128]{3,2,1,0:T(8,128)(2,1)S(1)}, u32[]{:S(2)}, u32[]{:S(2)}) %collective-permute-start.12) | collective-permute-done | bytes 262176 | tf_op jit(solution)/shard_map/ppermute | solution.py:18
  71.3 69.2 %while.10 = (s32[]{:T(128)}, f32[2,11,128,128]{3,2,1,0:T(8,128)}, s32[2,6]{1,0:T(2,128)S(1)}, s32[2]{0:T(128)S(1)}, s32[]{:T(128)}, /*index=5*/bf16[14,4,128,128...) while((s32[]{:T(128)}, f32[2,11,128,128]{3,2,1,0:T(8,128)}, s32[2,6]{1,0:T(2,128)S(1)}, ...), condition=%wide.region_3.4_spmd, body=%wide.region_0.3_spmd.sunk | while | flops 3967848448 | bytes 50824256 | solution.py:157
  72.7 3.1 %gather_fusion = bf16[6,4,128,128]{3,2,1,0:T(8,128)(2,1)} fusion(bf16[14,4,128,128]{3,2,1,0:T(8,128)(2,1)} %get-tuple-element.147, s32[1024]{0:T(1024)S(1)} %pad_clamp_fusion.5), kind=kCustom, calls=%fused_computation.clone.1 | custom fusion | bytes 1572888 | tf_op jit(solution)/shard_map/while/body/eval_jaxpr/gather | solution.py:51
  77.7 2.7 %copy.95 = f32[6,128,128,6]{1,0,2,3:T(8,128)} copy(f32[6,128,128,6]{2,3,1,0:T(8,128)S(1)} %fusion.123) | data formatting | bytes 4718592 | tf_op jit(solution)/shard_map/while/body/eval_jaxpr/str,srba->satb/dot_general | solution.py:71
  80.7 4.0 %multiply_reduce_fusion.2 = (f32[]{:T(128)}, f32[6,128,6,128]{3,0,1,2:T(8,128)S(1)}) fusion(f32[6]{0:T(128)S(1)} %get-tuple-element.112, s32[6,128]{1,0:T(8,128)S(1)} %multiply_add_fusion.2, s32[6,128]{0,1:T(8,128)S(1)} %copy.94, f32[6,128,128,6]{1,0,2,3:T(8,128)} %copy.95, pred[6,6,4,1]{0,2,3,1:T(4,128)(4,1)S(1)} %copy.96, ...), kind=kOutput, calls=%fused_computation.11.clone.1 | convolution fusion | flops 8847359 | bytes 5511340 | tf_op jit(solution)/shard_map/while/body/eval_jaxpr/str,trab->satb/dot_general | solution.py:65
  87.3 2.0 %copy.98 = bf16[6,128,6,128]{3,2,1,0:T(8,128)(2,1)} copy(bf16[6,128,6,128]{3,0,1,2:T(8,128)(2,1)S(1)} %divide_convert_fusion.2) | data formatting | bytes 2359296 | tf_op jit(solution)/shard_map/while/body/eval_jaxpr/convert_element_type | solution.py:86
  89.2 3.0 %copy.97 = f32[6,128,6,128]{3,2,1,0:T(8,128)} copy(f32[6,128,6,128]{3,0,1,2:T(8,128)S(1)} %get-tuple-element.119) | data formatting | bytes 4718592 | tf_op jit(solution)/shard_map/while/body/eval_jaxpr/add | solution.py:71
  92.3 4.9 %convolution_convert_fusion.4 = bf16[768,768]{1,0:T(8,128)(2,1)S(1)} fusion(f32[96,8,6,128]{3,2,1,0:T(8,128)} %bitcast.118, f32[]{:T(128)S(6)} %mul.120, f32[768]{0:T(1024)S(1)} %broadcast_bitcast_fusion.2, bf16[96,8,6,128]{3,2,1,0:T(8,128)(2,1)} %bitcast.119), kind=kOutput, calls=%fused_computation.22.clone.1 | convolution fusion | flops 1819017216 | bytes 4721668 | tf_op jit(solution)/shard_map/while/body/eval_jaxpr/dot_general | solution.py:46
  97.2 3.0 %convolution_convert_fusion.5 = bf16[768,768]{1,0:T(8,128)(2,1)} fusion(bf16[768,768]{1,0:T(8,128)(2,1)S(1)} %convolution_convert_fusion.4), kind=kOutput, calls=%fused_computation.21.clone.1 | convolution fusion | flops 1815478272 | bytes 2359296 | tf_op jit(solution)/shard_map/while/body/eval_jaxpr/dot_general | solution.py:46
  100.4 3.1 %fusion.124 = f32[768,128]{1,0:T(8,128)S(1)} fusion(bf16[768,768]{1,0:T(8,128)(2,1)} %convolution_convert_fusion.5, pred[768,768]{1,0:T(32,128)(4,1)S(1)} %iota_compare_fusion.4), kind=kOutput, calls=%fused_computation.27.clone.1 | convolution fusion | flops 302678016 | bytes 3145728 | tf_op jit(solution)/shard_map/while/body/eval_jaxpr/dot_general | solution.py:46
  107.3 3.1 %gather_fusion = bf16[6,4,128,128]{3,2,1,0:T(8,128)(2,1)} fusion(bf16[14,4,128,128]{3,2,1,0:T(8,128)(2,1)} %get-tuple-element.147, s32[1024]{0:T(1024)S(1)} %pad_clamp_fusion.5), kind=kCustom, calls=%fused_computation.clone.1 | custom fusion | bytes 1572888 | tf_op jit(solution)/shard_map/while/body/eval_jaxpr/gather | solution.py:51
  112.3 2.7 %copy.95 = f32[6,128,128,6]{1,0,2,3:T(8,128)} copy(f32[6,128,128,6]{2,3,1,0:T(8,128)S(1)} %fusion.123) | data formatting | bytes 4718592 | tf_op jit(solution)/shard_map/while/body/eval_jaxpr/str,srba->satb/dot_general | solution.py:71
  115.3 4.0 %multiply_reduce_fusion.2 = (f32[]{:T(128)}, f32[6,128,6,128]{3,0,1,2:T(8,128)S(1)}) fusion(f32[6]{0:T(128)S(1)} %get-tuple-element.112, s32[6,128]{1,0:T(8,128)S(1)} %multiply_add_fusion.2, s32[6,128]{0,1:T(8,128)S(1)} %copy.94, f32[6,128,128,6]{1,0,2,3:T(8,128)} %copy.95, pred[6,6,4,1]{0,2,3,1:T(4,128)(4,1)S(1)} %copy.96, ...), kind=kOutput, calls=%fused_computation.11.clone.1 | convolution fusion | flops 8847359 | bytes 5511340 | tf_op jit(solution)/shard_map/while/body/eval_jaxpr/str,trab->satb/dot_general | solution.py:65
  123.8 3.0 %copy.97 = f32[6,128,6,128]{3,2,1,0:T(8,128)} copy(f32[6,128,6,128]{3,0,1,2:T(8,128)S(1)} %get-tuple-element.119) | data formatting | bytes 4718592 | tf_op jit(solution)/shard_map/while/body/eval_jaxpr/add | solution.py:71
  126.9 4.9 %convolution_convert_fusion.4 = bf16[768,768]{1,0:T(8,128)(2,1)S(1)} fusion(f32[96,8,6,128]{3,2,1,0:T(8,128)} %bitcast.118, f32[]{:T(128)S(6)} %mul.120, f32[768]{0:T(1024)S(1)} %broadcast_bitcast_fusion.2, bf16[96,8,6,128]{3,2,1,0:T(8,128)(2,1)} %bitcast.119), kind=kOutput, calls=%fused_computation.22.clone.1 | convolution fusion | flops 1819017216 | bytes 4721668 | tf_op jit(solution)/shard_map/while/body/eval_jaxpr/dot_general | solution.py:46
  131.8 3.0 %convolution_convert_fusion.5 = bf16[768,768]{1,0:T(8,128)(2,1)} fusion(bf16[768,768]{1,0:T(8,128)(2,1)S(1)} %convolution_convert_fusion.4), kind=kOutput, calls=%fused_computation.21.clone.1 | convolution fusion | flops 1815478272 | bytes 2359296 | tf_op jit(solution)/shard_map/while/body/eval_jaxpr/dot_general | solution.py:46
  135.0 3.1 %fusion.124 = f32[768,128]{1,0:T(8,128)S(1)} fusion(bf16[768,768]{1,0:T(8,128)(2,1)} %convolution_convert_fusion.5, pred[768,768]{1,0:T(32,128)(4,1)S(1)} %iota_compare_fusion.4), kind=kOutput, calls=%fused_computation.27.clone.1 | convolution fusion | flops 302678016 | bytes 3145728 | tf_op jit(solution)/shard_map/while/body/eval_jaxpr/dot_general | solution.py:46
  140.5 2.0 %slice.101 = bf16[1,11,128,128]{3,2,1,0:T(8,128)(2,1)} slice(f32[2,11,128,128]{3,2,1,0:T(8,128)} %get-tuple-element.37), slice={[0:1], [0:11], [0:128], [0:128]} | slice | bytes 720896 | tf_op jit(solution)/shard_map/slice | solution.py:160
  142.5 6.5 %collective-permute-start.15 = (bf16[1,11,128,128]{3,2,1,0:T(8,128)(2,1)}, bf16[1,11,128,128]{3,2,1,0:T(8,128)(2,1)}, u32[]{:S(2)}, u32[]{:S(2)}) collective-permute-start(bf16[1,11,128,128]{3,2,1,0:T(8,128)(2,1)} %slice.101), channel_id=1, source_target_pairs={{1,0},{2,1},{3,2},{4,3},{5,4},{6,5},{7,6},{8,7},{9,8},{10,9},{11,1... | collective-permute-start | bytes 1081352 | tf_op jit(solution)/shard_map/ppermute | solution.py:18
  149.0 2.5 %gather_fusion.7 = bf16[2,128,128]{2,1,0:T(8,128)(2,1)} fusion(bf16[18,2,128,128]{3,2,1,0:T(8,128)(2,1)} %copy-done, s32[2]{0:T(128)S(1)} %copy-done.10), kind=kCustom, calls=%fused_computation.7 | custom fusion | bytes 131088 | tf_op jit(solution)/shard_map/gather | solution.py:108
  151.4 2.1 %gather_fusion.8 = bf16[26,128,128]{2,1,0:T(8,128)(2,1)S(1)} fusion(bf16[18,2,128,128]{3,2,1,0:T(8,128)(2,1)} %copy-done, s32[26]{0:T(128)S(1)} %copy-done.7), kind=kCustom, calls=%fused_computation.8 | custom fusion | bytes 1704144 | tf_op jit(solution)/shard_map/gather | solution.py:117
  159.3 2.2 %fusion.56 = f32[2,13,128,128]{3,2,1,0:T(8,128)} fusion(f32[2,13,128,128]{3,2,1,0:T(8,128)S(1)} %fusion.52, bf16[2,13,128,128]{3,2,1,0:T(8,128)(2,1)S(1)} %bitcast.122, f32[2,12,128,128]{3,2,1,0:T(8,128)S(1)} %convolution_add_fusion.1), kind=kOutput, calls=%fused_computation.87 | convolution fusion | flops 654737408 | bytes 5832704 | tf_op jit(solution)/shard_map/cpab,cpbd->cpad/dot_general | solution.py:120
  (135 shorter events, 48.9 us)
Async XLA Ops:
  1.8 32.7 %copy-start.12 = (s32[2]{0:T(128)S(1)}, s32[2]{0:T(128)}, u32[]{:S(2)}) copy-start(s32[2]{0:T(128)} %constant.241) | copy-start | bytes 28
  1.8 19.1 %collective-permute-start = (bf16[2,2,128,128]{3,2,1,0:T(8,128)(2,1)S(1)}, bf16[2,2,128,128]{3,2,1,0:T(8,128)(2,1)S(1)}, u32[]{:S(2)}, u32[]{:S(2)}) collective-permute-start(bf16[2,2,128,128]{3,2,1,0:T(8,128)(2,1)S(1)} %pad_maximum_fusion.1), channel_id=1, source_target_pairs={{0,4},{1,5},{2,6},{3,7},{4,8},{5,9},{6,10},{7,11},{8,12},{9,13},{1... | collective-permute-start | bytes 393224 | tf_op jit(solution)/shard_map/ppermute | solution.py:18
  5.9 16.4 %collective-permute-start.1 = (bf16[2,2,128,128]{3,2,1,0:T(8,128)(2,1)S(1)}, bf16[2,2,128,128]{3,2,1,0:T(8,128)(2,1)S(1)}, u32[]{:S(2)}, u32[]{:S(2)}) collective-permute-start(bf16[2,2,128,128]{3,2,1,0:T(8,128)(2,1)S(1)} %pad_maximum_fusion.1), channel_id=1, source_target_pairs={{0,3},{1,4},{2,5},{3,6},{4,7},{5,8},{6,9},{7,10},{8,11},{9,12},{10... | collective-permute-start | bytes 393224 | tf_op jit(solution)/shard_map/ppermute | solution.py:18
  9.9 13.7 %collective-permute-start.2 = (bf16[2,2,128,128]{3,2,1,0:T(8,128)(2,1)S(1)}, bf16[2,2,128,128]{3,2,1,0:T(8,128)(2,1)S(1)}, u32[]{:S(2)}, u32[]{:S(2)}) collective-permute-start(bf16[2,2,128,128]{3,2,1,0:T(8,128)(2,1)S(1)} %pad_maximum_fusion.1), channel_id=1, source_target_pairs={{0,2},{1,3},{2,4},{3,5},{4,6},{5,7},{6,8},{7,9},{8,10},{9,11},{10,... | collective-permute-start | bytes 393224 | tf_op jit(solution)/shard_map/ppermute | solution.py:18
  13.1 11.9 %collective-permute-start.3 = (bf16[2,2,128,128]{3,2,1,0:T(8,128)(2,1)S(1)}, bf16[2,2,128,128]{3,2,1,0:T(8,128)(2,1)S(1)}, u32[]{:S(2)}, u32[]{:S(2)}) collective-permute-start(bf16[2,2,128,128]{3,2,1,0:T(8,128)(2,1)S(1)} %pad_maximum_fusion.1), channel_id=1, source_target_pairs={{0,1},{1,2},{2,3},{3,4},{4,5},{5,6},{6,7},{7,8},{8,9},{9,10},{10,1... | collective-permute-start | bytes 393224 | tf_op jit(solution)/shard_map/ppermute | solution.py:18
  15.9 13.4 %collective-permute-start.4 = (bf16[2,2,128,128]{3,2,1,0:T(8,128)(2,1)S(1)}, bf16[2,2,128,128]{3,2,1,0:T(8,128)(2,1)S(1)}, u32[]{:S(2)}, u32[]{:S(2)}) collective-permute-start(bf16[2,2,128,128]{3,2,1,0:T(8,128)(2,1)S(1)} %pad_maximum_fusion.1), channel_id=1, source_target_pairs={{1,0},{2,1},{3,2},{4,3},{5,4},{6,5},{7,6},{8,7},{9,8},{10,9},{11,1... | collective-permute-start | bytes 393224 | tf_op jit(solution)/shard_map/ppermute | solution.py:18
  18.5 16.7 %copy-start.11 = (s32[2]{0:T(128)S(1)}, s32[2]{0:T(128)}, u32[]{:S(2)}) copy-start(s32[2]{0:T(128)} %constant.232) | copy-start | bytes 28
  20.9 8.4 %collective-permute-start.5 = (bf16[2,2,128,128]{3,2,1,0:T(8,128)(2,1)S(1)}, bf16[2,2,128,128]{3,2,1,0:T(8,128)(2,1)S(1)}, u32[]{:S(2)}, u32[]{:S(2)}) collective-permute-start(bf16[2,2,128,128]{3,2,1,0:T(8,128)(2,1)S(1)} %pad_maximum_fusion.1), channel_id=1, source_target_pairs={{2,0},{3,1},{4,2},{5,3},{6,4},{7,5},{8,6},{9,7},{10,8},{11,9},{12,... | collective-permute-start | bytes 393224 | tf_op jit(solution)/shard_map/ppermute | solution.py:18
  22.3 10.0 %collective-permute-start.6 = (bf16[2,2,128,128]{3,2,1,0:T(8,128)(2,1)S(1)}, bf16[2,2,128,128]{3,2,1,0:T(8,128)(2,1)S(1)}, u32[]{:S(2)}, u32[]{:S(2)}) collective-permute-start(bf16[2,2,128,128]{3,2,1,0:T(8,128)(2,1)S(1)} %pad_maximum_fusion.1), channel_id=1, source_target_pairs={{3,0},{4,1},{5,2},{6,3},{7,4},{8,5},{9,6},{10,7},{11,8},{12,9},{13... | collective-permute-start | bytes 393224 | tf_op jit(solution)/shard_map/ppermute | solution.py:18
  23.6 11.0 %collective-permute-start.7 = (bf16[2,2,128,128]{3,2,1,0:T(8,128)(2,1)S(1)}, bf16[2,2,128,128]{3,2,1,0:T(8,128)(2,1)S(1)}, u32[]{:S(2)}, u32[]{:S(2)}) collective-permute-start(bf16[2,2,128,128]{3,2,1,0:T(8,128)(2,1)S(1)} %pad_maximum_fusion.1), channel_id=1, source_target_pairs={{4,0},{5,1},{6,2},{7,3},{8,4},{9,5},{10,6},{11,7},{12,8},{13,9},{1... | collective-permute-start | bytes 393224 | tf_op jit(solution)/shard_map/ppermute | solution.py:18
  24.9 11.8 %collective-permute-start.8 = (bf16[1,5,128,128]{3,2,1,0:T(8,128)(2,1)S(1)}, bf16[1,5,128,128]{3,2,1,0:T(8,128)(2,1)S(1)}, u32[]{:S(2)}, u32[]{:S(2)}) collective-permute-start(bf16[1,5,128,128]{3,2,1,0:T(8,128)(2,1)S(1)} %slice.77), channel_id=1, source_target_pairs={{0,1},{1,2},{2,3},{3,4},{4,5},{5,6},{6,7},{7,8},{8,9},{9,10},{10,1... | collective-permute-start | bytes 491528 | tf_op jit(solution)/shard_map/ppermute | solution.py:18
  34.6 2.8 %copy-start = (bf16[18,2,128,128]{3,2,1,0:T(8,128)(2,1)}, bf16[18,2,128,128]{3,2,1,0:T(8,128)(2,1)S(1)}, u32[]{:S(2)}) copy-start(bf16[18,2,128,128]{3,2,1,0:T(8,128)(2,1)S(1)} %constant_dynamic-update-slice_fusion) | copy-start | bytes 3538948
  38.9 12.7 %collective-permute-start.9 = (bf16[2,4,128,128]{3,2,1,0:T(8,128)(2,1)S(1)}, bf16[2,4,128,128]{3,2,1,0:T(8,128)(2,1)S(1)}, u32[]{:S(2)}, u32[]{:S(2)}) collective-permute-start(bf16[2,4,128,128]{3,2,1,0:T(8,128)(2,1)S(1)} %fusion.64), channel_id=1, source_target_pairs={{0,3},{1,4},{2,5},{3,6},{4,7},{5,8},{6,9},{7,10},{8,11},{9,12},{10... | collective-permute-start | bytes 786440 | tf_op jit(solution)/shard_map/ppermute | solution.py:18
  42.6 11.2 %collective-permute-start.10 = (bf16[2,4,128,128]{3,2,1,0:T(8,128)(2,1)S(1)}, bf16[2,4,128,128]{3,2,1,0:T(8,128)(2,1)S(1)}, u32[]{:S(2)}, u32[]{:S(2)}) collective-permute-start(bf16[2,4,128,128]{3,2,1,0:T(8,128)(2,1)S(1)} %fusion.64), channel_id=1, source_target_pairs={{0,2},{1,3},{2,4},{3,5},{4,6},{5,7},{6,8},{7,9},{8,10},{9,11},{10,... | collective-permute-start | bytes 786440 | tf_op jit(solution)/shard_map/ppermute | solution.py:18
  45.4 9.2 %collective-permute-start.11 = (bf16[2,4,128,128]{3,2,1,0:T(8,128)(2,1)S(1)}, bf16[2,4,128,128]{3,2,1,0:T(8,128)(2,1)S(1)}, u32[]{:S(2)}, u32[]{:S(2)}) collective-permute-start(bf16[2,4,128,128]{3,2,1,0:T(8,128)(2,1)S(1)} %fusion.64), channel_id=1, source_target_pairs={{0,1},{1,2},{2,3},{3,4},{4,5},{5,6},{6,7},{7,8},{8,9},{9,10},{10,1... | collective-permute-start | bytes 786440 | tf_op jit(solution)/shard_map/ppermute | solution.py:18
  48.4 19.2 %collective-permute-start.12 = (bf16[2,4,128,128]{3,2,1,0:T(8,128)(2,1)S(1)}, bf16[2,4,128,128]{3,2,1,0:T(8,128)(2,1)S(1)}, u32[]{:S(2)}, u32[]{:S(2)}) collective-permute-start(bf16[2,4,128,128]{3,2,1,0:T(8,128)(2,1)S(1)} %fusion.64), channel_id=1, source_target_pairs={{1,0},{2,1},{3,2},{4,3},{5,4},{6,5},{7,6},{8,7},{9,8},{10,9},{11,1... | collective-permute-start | bytes 786440 | tf_op jit(solution)/shard_map/ppermute | solution.py:18
  50.3 19.5 %collective-permute-start.13 = (bf16[2,4,128,128]{3,2,1,0:T(8,128)(2,1)S(1)}, bf16[2,4,128,128]{3,2,1,0:T(8,128)(2,1)S(1)}, u32[]{:S(2)}, u32[]{:S(2)}) collective-permute-start(bf16[2,4,128,128]{3,2,1,0:T(8,128)(2,1)S(1)} %fusion.64), channel_id=1, source_target_pairs={{2,0},{3,1},{4,2},{5,3},{6,4},{7,5},{8,6},{9,7},{10,8},{11,9},{12,... | collective-permute-start | bytes 786440 | tf_op jit(solution)/shard_map/ppermute | solution.py:18
  51.6 18.9 %collective-permute-start.14 = (bf16[2,4,128,128]{3,2,1,0:T(8,128)(2,1)S(1)}, bf16[2,4,128,128]{3,2,1,0:T(8,128)(2,1)S(1)}, u32[]{:S(2)}, u32[]{:S(2)}) collective-permute-start(bf16[2,4,128,128]{3,2,1,0:T(8,128)(2,1)S(1)} %fusion.64), channel_id=1, source_target_pairs={{3,0},{4,1},{5,2},{6,3},{7,4},{8,5},{9,6},{10,7},{11,8},{12,9},{13... | collective-permute-start | bytes 786440 | tf_op jit(solution)/shard_map/ppermute | solution.py:18
  53.9 17.4 %copy-start.9 = (s32[2,6]{1,0:T(2,128)S(1)}, s32[2,6]{1,0:T(2,128)}, u32[]{:S(2)}) copy-start(s32[2,6]{1,0:T(2,128)} %param.27) | copy-start | bytes 148
  71.3 77.7 %copy-start.10 = (s32[2]{0:T(128)S(1)}, s32[2]{0:T(128)}, u32[]{:S(2)}) copy-start(s32[2]{0:T(128)} %constant.249) | copy-start | bytes 28
  71.3 80.2 %copy-start.7 = (s32[26]{0:T(128)S(1)}, s32[26]{0:T(128)}, u32[]{:S(2)}) copy-start(s32[26]{0:T(128)} %constant.257) | copy-start | bytes 316
  100.4 4.0 %copy-start.2 = (f32[2,11,128,128]{3,2,1,0:T(8,128)S(1)}, f32[2,11,128,128]{3,2,1,0:T(8,128)}, u32[]{:S(2)}) copy-start(f32[2,11,128,128]{3,2,1,0:T(8,128)} %get-tuple-element.133) | copy-start | bytes 4325380 | tf_op jit(solution)/shard_map/while
  104.7 1.2 copy-start.3
  135.0 4.0 %copy-start.2 = (f32[2,11,128,128]{3,2,1,0:T(8,128)S(1)}, f32[2,11,128,128]{3,2,1,0:T(8,128)}, u32[]{:S(2)}) copy-start(f32[2,11,128,128]{3,2,1,0:T(8,128)} %get-tuple-element.133) | copy-start | bytes 4325380 | tf_op jit(solution)/shard_map/while
  139.3 1.2 copy-start.3
  140.5 13.1 %copy-start.1 = (bf16[18,2,128,128]{3,2,1,0:T(8,128)(2,1)S(1)}, bf16[18,2,128,128]{3,2,1,0:T(8,128)(2,1)}, u32[]{:S(2)}) copy-start(bf16[18,2,128,128]{3,2,1,0:T(8,128)(2,1)} %copy-done) | copy-start | bytes 3538948
  140.5 13.1 %copy-start.6 = (s32[26]{0:T(128)S(1)}, s32[26]{0:T(128)}, u32[]{:S(2)}) copy-start(s32[26]{0:T(128)} %constant.223) | copy-start | bytes 316
  142.5 12.8 %collective-permute-start.15 = (bf16[1,11,128,128]{3,2,1,0:T(8,128)(2,1)}, bf16[1,11,128,128]{3,2,1,0:T(8,128)(2,1)}, u32[]{:S(2)}, u32[]{:S(2)}) collective-permute-start(bf16[1,11,128,128]{3,2,1,0:T(8,128)(2,1)} %slice.101), channel_id=1, source_target_pairs={{1,0},{2,1},{3,2},{4,3},{5,4},{6,5},{7,6},{8,7},{9,8},{10,9},{11,1... | collective-permute-start | bytes 1081352 | tf_op jit(solution)/shard_map/ppermute | solution.py:18
  151.4 3.8 %copy-start.4 = (f32[2,11,128,128]{3,2,1,0:T(8,128)S(1)}, f32[2,11,128,128]{3,2,1,0:T(8,128)}, u32[]{:S(2)}) copy-start(f32[2,11,128,128]{3,2,1,0:T(8,128)} %get-tuple-element.37) | copy-start | bytes 4325380
  155.3 1.1 copy-start.8
  158.1 1.2 copy-start.5
where the time goes:
time: 164 us; the launch traced here: 162 us
  starting transfers between devices  44.6 us (27%)
  local copies, waits for them, and re-layouts  43.2 us (26%)
  matrix products  41.5 us (25%)
  waiting for transfers between devices  18.2 us (11%)
  other arithmetic  10.7 us (7%)
  loops' own time  2.72 us (2%)
    ppermute x16, starting transfers between devices, shifted_2(): return lax.ppermute(value, axis, pairs)  44.6 us
    dot_general x6, matrix products, mat_product(): return jnp.dot(left, right, preferred_element_type=jnp.float32)  22 us
    ppermute x16, waiting for transfers between devices, shifted_2(): return lax.ppermute(value, axis, pairs)  18.2 us
    dot_general x2, matrix products, solve_column(): jnp.einsum('str,trab->satb', lower_sel.astype(jnp.bfloat16), gathered, pr...  8.04 us
    gather x2, local copies, waits for them, and re-layouts, solve_column(): gathered = orth_ext[positions]  6.1 us
    add x2, local copies, waits for them, and re-layouts, solve_column(): sub_block + jnp.einsum('str,srba->satb', upper_sel.astype(jnp.bfloat16),...  6.09 us
    dot_general x2, local copies, waits for them, and re-layouts, solve_column(): jnp.einsum('str,srba->satb', upper_sel.astype(jnp.bfloat16), gathered, pr...  5.38 us
    unnamed x35, local copies, waits for them, and re-layouts  4.68 us
  transfers between devices with their start and end apart: 16, of which 4 were waited for; matrix products, arithmetic and copies ran while one was open for 10% of the time, Pallas kernels for 0%

commit v1 on v0

v1 whole, which is shorter than its diff:
```python
import functools
import math

import jax
import jax.numpy as jnp
from jax import lax
from jax.experimental import pallas as pl
from jax.experimental.pallas import tpu as pltpu
from jax.sharding import PartitionSpec as P

RO = 3
Q = 5
STEPS = 3
CHEM = 0.25
AXES = ("space", "inner")
MESH = pl.DeviceIdType.MESH
BF = jnp.bfloat16
F32 = jnp.float32
PER = 5
REACH = 3
HALF = 5
VMEM_LIMIT = 60 * 1024 * 1024


def gather_kernel(total, inner, pay_ref, out_ref, own_sem, send_sem, recv_sem):
    me = lax.axis_index("space") * inner + lax.axis_index("inner")
    core = lax.rem(me, 2)
    partner = me + 1 - 2 * core
    far = jnp.where(core == 1, me + 3, me - 3)
    has_low = me >= 2
    has_high = me + 2 < total
    has_far = (far >= 0) & (far < total)

    def place(device):
        return (device // inner, lax.rem(device, inner))

    barrier = pltpu.get_barrier_semaphore()

    def greet(device):
        pl.semaphore_signal(barrier, inc=1, device_id=place(device), device_id_type=MESH)

    greet(partner)
    pl.when(has_low)(lambda: greet(me - 2))
    pl.when(has_high)(lambda: greet(me + 2))
    pl.when(has_far)(lambda: greet(far))

    own = pltpu.make_async_copy(pay_ref, out_ref.at[REACH], own_sem)
    own.start()
    for slot in range(2 * REACH + 1):
        if slot != REACH:
            source = me + slot - REACH

            @pl.when((source < 0) | (source >= total))
            def _():
                out_ref[slot] = jnp.zeros(out_ref.shape[1:], out_ref.dtype)

    peers = 1 + has_low.astype(jnp.int32) + has_high.astype(jnp.int32) + has_far.astype(jnp.int32)
    pl.semaphore_wait(barrier, peers)

    def copy(src, dst_slot, lo, hi, number, part, device):
        return pltpu.make_async_remote_copy(
            src_ref=src.at[pl.ds(lo, hi - lo)],
            dst_ref=out_ref.at[dst_slot, pl.ds(lo, hi - lo)],
            send_sem=send_sem.at[number, part],
            recv_sem=recv_sem.at[dst_slot, part],
            device_id=place(device),
            device_id_type=MESH,
        )

    halves = ((0, 0, HALF), (1, HALF, 2 * HALF))

    up = [copy(pay_ref, 1, lo, hi, 0, part, me + 2) for part, lo, hi in halves]
    down = [copy(pay_ref, 5, lo, hi, 1, part, me - 2) for part, lo, hi in halves]
    far_up = [copy(pay_ref, 0, lo, hi, 2, part, far) for part, lo, hi in ((0, 2, HALF), (1, HALF, 10))]
    far_down = [copy(pay_ref, 6, lo, hi, 2, part, far) for part, lo, hi in ((0, 0, HALF), (1, HALF, 7))]
    side_up = [copy(pay_ref, 2, lo, hi, 3, part, partner) for part, lo, hi in halves]
    side_down = [copy(pay_ref, 4, lo, hi, 3, part, partner) for part, lo, hi in halves]
    low0 = [copy(out_ref.at[1], 0, lo, hi, 4, part, partner) for part, lo, hi in ((0, 2, HALF), (1, HALF, 10))]
    low1 = [copy(out_ref.at[1], 2, lo, hi, 4, part, partner) for part, lo, hi in halves]
    high0 = [copy(out_ref.at[5], 4, lo, hi, 5, part, partner) for part, lo, hi in halves]
    high1 = [copy(out_ref.at[5], 6, lo, hi, 5, part, partner) for part, lo, hi in ((0, 0, HALF), (1, HALF, 7))]

    even = core == 0
    odd = core == 1
    for part in range(2):
        pl.when(has_high)(lambda: up[part].start())
        pl.when(has_low)(lambda: down[part].start())
        pl.when(has_far & odd)(lambda: far_up[part].start())
        pl.when(has_far & even)(lambda: far_down[part].start())
        pl.when(even)(lambda: side_up[part].start())
        pl.when(odd)(lambda: side_down[part].start())

    for part in range(2):

        @pl.when(has_low)
        def _():
            up[part].wait_recv()
            pl.when(even)(lambda: low0[part].start())
            pl.when(odd)(lambda: low1[part].start())

        @pl.when(has_high)
        def _():
            down[part].wait_recv()
            pl.when(even)(lambda: high0[part].start())
            pl.when(odd)(lambda: high1[part].start())

    for part in range(2):

        @pl.when(even)
        def _():
            pl.when(has_far)(lambda: far_up[part].wait_recv())
            pl.when(has_low)(lambda: low1[part].wait_recv())
            side_down[part].wait_recv()
            pl.when(has_high)(lambda: high1[part].wait_recv())
            pl.when(has_far)(lambda: far_down[part].wait_send())
            side_up[part].wait_send()
            pl.when(has_low)(lambda: low0[part].wait_send())
            pl.when(has_high)(lambda: high0[part].wait_send())

        @pl.when(odd)
        def _():
            pl.when(has_low)(lambda: low0[part].wait_recv())
            side_up[part].wait_recv()
            pl.when(has_high)(lambda: high0[part].wait_recv())
            pl.when(has_far)(lambda: far_down[part].wait_recv())
            pl.when(has_far)(lambda: far_up[part].wait_send())
            side_down[part].wait_send()
            pl.when(has_low)(lambda: low1[part].wait_send())
            pl.when(has_high)(lambda: high1[part].wait_send())

        pl.when(has_high)(lambda: up[part].wait_send())
        pl.when(has_low)(lambda: down[part].wait_send())
    own.wait()


def gather(payload, total, inner):
    shape = (2 * REACH + 1,) + payload.shape
    return pl.pallas_call(
        functools.partial(gather_kernel, total, inner),
        out_shape=jax.ShapeDtypeStruct(shape, payload.dtype),
        in_specs=[pl.BlockSpec(memory_space=pltpu.VMEM)],
        out_specs=pl.BlockSpec(memory_space=pltpu.VMEM),
        scratch_shapes=[
            pltpu.SemaphoreType.DMA,
            pltpu.SemaphoreType.DMA((6, 2)),
            pltpu.SemaphoreType.DMA((2 * REACH + 1, 2)),
        ],
        compiler_params=pltpu.CompilerParams(collective_id=0, has_side_effects=True),
        name="gather",
    )(payload)


def block_of(g_ref, column, which):
    index = column + 2 * REACH
    return g_ref[index // 2, (index % 2) * PER + which]


def dot(left, right):
    return jnp.dot(left, right, preferred_element_type=F32)


def eye_mask(rows, columns, shift=0):
    row = lax.broadcasted_iota(jnp.int32, (rows, columns), 0) + shift
    return row == lax.broadcasted_iota(jnp.int32, (rows, columns), 1)


def fold(square):
    n = square.shape[0]
    return jnp.sum(square.reshape(n // 8, 8, square.shape[1]), axis=0)


def orth_stage(g_ref, h_ref, sq_ref, zt_ref):
    bs = g_ref.shape[-1]
    last = Q + 1
    quarter = jnp.where(eye_mask(bs, bs), CHEM, 0.0)
    for a in range(-Q, last + 1):
        zt_ref[a + Q] = jnp.concatenate(
            [block_of(g_ref, a, 0).T, block_of(g_ref, a, 1).T], axis=1
        )
    for b in range(-Q, last + 1):
        count = min(RO + 1, last - b + 1)
        z_col = jnp.concatenate([block_of(g_ref, b, 0), block_of(g_ref, b, 1)], axis=0)
        below = block_of(g_ref, b - 1, 3)
        rows = [jnp.concatenate([block_of(g_ref, b - 1, 2), below.T], axis=1)]
        rows.append(jnp.concatenate([below, block_of(g_ref, b, 2)], axis=1))
        if count >= 2:
            rows.append(jnp.concatenate([block_of(g_ref, b - 1, 4), block_of(g_ref, b, 3)], axis=1))
        product = dot(jnp.concatenate(rows, axis=0), z_col).astype(BF)
        if count >= 3:
            tail = dot(block_of(g_ref, b, 4), z_col[bs:]).astype(BF)
            product = jnp.concatenate([product, tail], axis=0)
        for off in range(count):
            transposed = zt_ref[b + off + Q]
            if off < RO:
                value = dot(transposed, product[off * bs : (off + 2) * bs])
            else:
                value = dot(transposed[:, :bs], product[off * bs : (off + 1) * bs])
            value = value.astype(BF)
            h_ref[b + Q, off] = value
            wide = value.astype(F32)
            if off == 0:
                wide = quarter - wide
            sq_ref[b + Q, off] = fold(wide * wide)


def solve_stage(which, lists_ref, first, h_ref, sq_ref, band_ref, x_ref, m_ref, y_ref):
    bs = h_ref.shape[-1]
    slot_count = lists_ref.shape[1]
    order = slot_count * bs
    slots = [lists_ref[which, s] for s in range(slot_count)]
    live = [slot >= 0 for slot in slots]
    place = [jnp.clip(slot - first + Q, 0, 2 * Q + 1) for slot in slots]
    total = jnp.zeros((8, bs), F32)
    live_count = jnp.int32(0)
    pick = {}
    for s in range(slot_count):
        live_count = live_count + live[s].astype(jnp.int32)
        for t in range(s + 1):
            low = jnp.minimum(place[s], place[t])
            off = jnp.maximum(place[s], place[t]) - low
            valid = live[s] & live[t] & (off <= RO)
            off = jnp.minimum(off, RO)
            pick[s, t] = (low, off, valid)
            part = jnp.where(valid, sq_ref[low, off], 0.0)
            total = total + (part if s == t else 2.0 * part)
    total = jnp.sum(jnp.sum(total, axis=1, keepdims=True), axis=0, keepdims=True)
    rows = jnp.full((1, 1), live_count * bs, jnp.int32).astype(F32)
    scale = 2.0 * jnp.sqrt(total / rows + 1e-06)
    inverse = 1.0 / scale
    eye = eye_mask(bs, bs)
    for s in range(slot_count):
        for t in range(s + 1):
            low, off, valid = pick[s, t]
            value = h_ref[low, off].astype(F32)
            if s == t:
                value = jnp.where(eye, CHEM, 0.0) - value
            else:
                value = -value
            value = jnp.where(valid, value * inverse, 0.0)
            here, there = pl.ds(s * bs, bs), pl.ds(t * bs, bs)
            if s == t:
                x_ref[here, here] = value.astype(BF)
            else:
                flipped = value.T
                straight = place[s] >= place[t]
                x_ref[here, there] = jnp.where(straight, value, flipped).astype(BF)
                x_ref[there, here] = jnp.where(straight, flipped, value).astype(BF)
    chunk = math.gcd(order, 256)
    source, target = x_ref, y_ref
    for step in range(STEPS - 1):
        for at in range(0, order, chunk):
            square = dot(source[pl.ds(at, chunk), :], source[...])
            unit = jnp.where(eye_mask(chunk, order, at), 1.5, 0.0)
            m_ref[pl.ds(at, chunk), :] = (unit - 0.5 * square).astype(BF)
        for at in range(0, order, chunk):
            target[pl.ds(at, chunk), :] = dot(source[pl.ds(at, chunk), :], m_ref[...]).astype(BF)
        source, target = target, source
    columns = source[:, :bs]
    for at in range(0, order, chunk):
        square = dot(source[pl.ds(at, chunk), :], columns)
        unit = jnp.where(eye_mask(chunk, bs, at), 1.5, 0.0)
        m_ref[pl.ds(at, chunk), :bs] = (unit - 0.5 * square).astype(BF)
    factor = m_ref[:, :bs]
    for r in range(2 * Q + 1):
        band_ref[r] = jnp.zeros((bs, bs), band_ref.dtype)
    for s in range(slot_count):
        result = dot(source[pl.ds(s * bs, bs), :], factor)
        if s == 0:
            result = result + jnp.where(eye, 1.0, 0.0)
        row = jnp.clip(slots[s] - first - which + Q, 0, 2 * Q)

        @pl.when(live[s])
        def _():
            band_ref[row] = (0.5 * result).astype(band_ref.dtype)


def first_index(inner, local_count):
    return (lax.axis_index("space") * inner + lax.axis_index("inner")) * local_count


def first_kernel(inner, lists_ref, g_ref, h_ref, sq_ref, band_ref, zt_ref, x_ref, m_ref, y_ref):
    orth_stage(g_ref, h_ref, sq_ref, zt_ref)
    first = first_index(inner, lists_ref.shape[0])
    solve_stage(0, lists_ref, first, h_ref, sq_ref, band_ref, x_ref, m_ref, y_ref)


def second_kernel(inner, lists_ref, h_ref, sq_ref, band_ref, x_ref, m_ref, y_ref):
    first = first_index(inner, lists_ref.shape[0])
    solve_stage(1, lists_ref, first, h_ref, sq_ref, band_ref, x_ref, m_ref, y_ref)


def back_kernel(g_ref, band0_ref, band1_ref, next_ref, out_ref):
    bs = g_ref.shape[-1]
    zero = jnp.zeros((bs, bs), BF)
    for column in range(2):
        mine = (band0_ref, band1_ref)[column]
        after = (band1_ref, next_ref)[column]
        right = jnp.concatenate(
            [block_of(g_ref, column, 1).T, block_of(g_ref, column + 1, 0).T], axis=0
        )
        rows = []
        for i in range(2 * Q + 2):
            here = mine[i] if i <= 2 * Q else zero
            there = after[i - 1] if i >= 1 else zero
            rows.append(jnp.concatenate([here, there], axis=1))
        y = dot(jnp.concatenate(rows, axis=0), right).astype(BF)
        for p in range(2 * Q + 3):
            a = column + p - Q - 1
            if p == 0:
                value = dot(block_of(g_ref, a + 1, 0), y[:bs])
            elif p == 2 * Q + 2:
                value = dot(block_of(g_ref, a, 1), y[(p - 1) * bs : p * bs])
            else:
                left = jnp.concatenate(
                    [block_of(g_ref, a, 1), block_of(g_ref, a + 1, 0)], axis=1
                )
                value = dot(left, y[(p - 1) * bs : (p + 1) * bs])
            out_ref[column, p] = value


def vmem():
    return pl.BlockSpec(memory_space=pltpu.VMEM)


def smem():
    return pl.BlockSpec(memory_space=pltpu.SMEM)


def local(total, inner, hamiltonian, pattern, ortho, lists):
    local_count, _, bs = hamiltonian.shape[:3]
    slot_count = lists.shape[1]
    order = slot_count * bs
    first = lax.axis_index(AXES) * local_count
    columns = first + jnp.arange(local_count, dtype=jnp.int32)
    masked = hamiltonian[:, 2:] * pattern[:, 2:, None, None].astype(BF)
    upper = jnp.where((columns == 0)[:, None, None], jnp.zeros_like(ortho[:, 0]), ortho[:, 0])
    diagonal = (jnp.eye(bs, dtype=F32) + ortho[:, 1].astype(F32)).astype(BF)
    payload = jnp.concatenate([upper[:, None], diagonal[:, None], masked], axis=1)
    payload = payload.reshape(local_count * PER, bs, bs)
    gathered = gather(payload, total, inner)

    params = pltpu.CompilerParams(vmem_limit_bytes=VMEM_LIMIT)
    band_shape = jax.ShapeDtypeStruct((2 * Q + 1, bs, bs), BF)
    work = [pltpu.VMEM((order, order), BF)] * 3
    orth_cols = 2 * Q + local_count
    flops = 2 * order**3 * 5
    cost = pl.CostEstimate(flops=flops, bytes_accessed=4 << 20, transcendentals=0)
    h, sq, band0 = pl.pallas_call(
        functools.partial(first_kernel, inner),
        out_shape=(
            jax.ShapeDtypeStruct((orth_cols, RO + 1, bs, bs), BF),
            jax.ShapeDtypeStruct((orth_cols, RO + 1, 8, bs), F32),
            band_shape,
        ),
        in_specs=[smem(), vmem()],
        out_specs=(vmem(), vmem(), vmem()),
        scratch_shapes=[pltpu.VMEM((orth_cols, bs, 2 * bs), BF)] + work,
        compiler_params=params,
        cost_estimate=cost,
        name="first",
    )(lists, gathered)
    devices = total
    pairs = [(i, i - 1) for i in range(1, devices)]
    following = lax.ppermute(band0, AXES, pairs)
    band1 = pl.pallas_call(
        functools.partial(second_kernel, inner),
        out_shape=band_shape,
        in_specs=[smem(), vmem(), vmem()],
        out_specs=vmem(),
        scratch_shapes=work,
        compiler_params=params,
        cost_estimate=cost,
        name="second",
    )(lists, h, sq)
    return pl.pallas_call(
        back_kernel,
        out_shape=jax.ShapeDtypeStruct((local_count, 2 * Q + 3, bs, bs), F32),
        in_specs=[vmem()] * 4,
        out_specs=vmem(),
        compiler_params=params,
        name="back",
    )(gathered, band0, band1, following)


def solution(mesh):
    in_specs = (
        P(AXES, None, None, None),
        P(AXES, None),
        P(AXES, None, None, None),
        P(AXES, None),
    )
    inner = mesh.shape["inner"]
    total = mesh.shape["space"] * inner
    return jax.shard_map(
        functools.partial(local, total, inner),
        mesh=mesh,
        in_specs=in_specs,
        out_specs=P(AXES, None, None, None),
        check_vma=False,
    )
```

time: 164 us -> 57.8 us (0.35)
  the two profiles are of different devices: /device:TPU:1 before, /device:TPU:4 now
where the time goes in v1:
time: 57.8 us; the launch traced here: 57.5 us
  Pallas kernels  46.5 us (80%)
  starting transfers between devices  5.83 us (10%)
  other arithmetic  4.25 us (7%)
  local copies, waits for them, and re-layouts  0.84 us (1%)
    pallas_call x1, Pallas kernels, gather(): pl.pallas_call(functools.partial(gather_kernel, total, inner), out_shape=...  22 us
    pallas_call x1, Pallas kernels, local(): pl.pallas_call(functools.partial(first_kernel, inner), out_shape=(jax.Sha...  12.1 us
    pallas_call x1, Pallas kernels, local(): pl.pallas_call(functools.partial(second_kernel, inner), out_shape=band_sh...  8.12 us
    ppermute x1, starting transfers between devices, local(): following = lax.ppermute(band0, AXES, pairs)  5.83 us
    pallas_call x1, Pallas kernels, local(): pl.pallas_call(back_kernel, out_shape=jax.ShapeDtypeStruct((local_count,...  4.27 us
  transfers between devices with their start and end apart: 1, of which 0 were waited for; matrix products, arithmetic and copies ran while one was open for 0% of the time, Pallas kernels for 14%

profile of v1, /device:TPU:4, one launch (start us, length us, event | category | flops | bytes accessed | tf_op | source)
XLA Modules:
  0.0 57.5 jit_solution(8054969113263113514)
XLA Ops:
  0.0 0.7 %convert.3 = bf16[2,5]{1,0:T(2,128)(2,1)S(1)} convert(s32[2,5]{1,0:T(2,128)} %param.5) | non-fusion elementwise | flops 10 | bytes 60 | tf_op jit(solution)/shard_map/convert
  0.7 0.1 slice.16
  0.8 0.9 %slice_select_fusion = bf16[2,1,128,128]{3,2,1,0:T(8,128)(2,1)S(1)} fusion(bf16[2,2,128,128]{3,2,1,0:T(8,128)(2,1)} %param.6, pred[2]{0:T(512)(128)(4,1)S(1)} %add_compare_fusion), kind=kLoop, calls=%fused_computation.4 | loop fusion | flops 32768 | bytes 131074 | tf_op jit(solution)/shard_map/jit(_where)/select_n | solution.py:336
  1.7 0.9 %add_convert_fusion = bf16[2,1,128,128]{3,2,1,0:T(8,128)(2,1)S(1)} fusion(bf16[2,2,128,128]{3,2,1,0:T(8,128)(2,1)} %param.6, f32[128,128]{1,0:T(8,128)S(1)} %fusion), kind=kLoop, calls=%fused_computation.2 | loop fusion | flops 98304 | bytes 196608 | tf_op jit(solution)/shard_map/convert_element_type | solution.py:337
  2.6 1.0 %slice_multiply_fusion = bf16[2,3,128,128]{3,2,1,0:T(8,128)(2,1)S(1)} fusion(bf16[2,5,128,128]{3,2,1,0:T(8,128)(2,1)} %param.4, bf16[2,3]{1,0:T(2,128)(2,1)S(1)} %slice.16), kind=kLoop, calls=%fused_computation.1 | loop fusion | flops 98304 | bytes 393228 | tf_op jit(solution)/shard_map/mul | solution.py:335
  3.6 0.8 %pad_maximum_fusion = bf16[2,5,128,128]{3,2,1,0:T(8,128)(2,1)} fusion(bf16[2,3,128,128]{3,2,1,0:T(8,128)(2,1)S(1)} %slice_multiply_fusion, bf16[2,1,128,128]{3,2,1,0:T(8,128)(2,1)S(1)} %add_convert_fusion, bf16[2,1,128,128]{3,2,1,0:T(8,128)(2,1)S(1)} %slice_select_fusion), kind=kLoop, calls=%fused_computation | loop fusion | flops 327680 | bytes 655360 | tf_op jit(solution)/shard_map/concatenate | solution.py:338
  4.3 22.0 %gather.1.g_ref = bf16[7,10,128,128]{3,2,1,0:T(8,128)(2,1)} custom-call(bf16[10,128,128]{2,1,0:T(8,128)(2,1)} %bitcast.1), custom_call_target="tpu_custom_call" | custom-call | tf_op jit(solution)/shard_map/gather/pallas_call | solution.py:138
  26.4 12.1 %first.1 = (bf16[12,4,128,128]{3,2,1,0:T(8,128)(2,1)}, f32[12,4,8,128]{3,2,1,0:T(8,128)}, bf16[11,128,128]{2,1,0:T(8,128)(2,1)}) custom-call(s32[2,6]{1,0:T(2,128)} %lists_ref.3, bf16[7,10,128,128]{3,2,1,0:T(8,128)(2,1)} %gather.1.g_ref), custom_call_target="tpu_custom_call" | custom-call | flops 4529848320 | bytes 4194304 | tf_op jit(solution)/shard_map/first/pallas_call | solution.py:348
  38.5 5.8 %collective-permute-start = (bf16[11,128,128]{2,1,0:T(8,128)(2,1)}, bf16[11,128,128]{2,1,0:T(8,128)(2,1)S(1)}, u32[]{:S(2)}, u32[]{:S(2)}) collective-permute-start(bf16[11,128,128]{2,1,0:T(8,128)(2,1)} %get-tuple-element.8.band0_ref), channel_id=1, source_target_pairs={{1,0},{2,1},{3,2},{4,3},{5,4},{6,5},{7,6},{8,7},{9,8},{10,9},{11,1... | collective-permute-start | bytes 1081352 | tf_op jit(solution)/shard_map/ppermute | solution.py:364
  44.3 8.1 %second.1.band1_ref = bf16[11,128,128]{2,1,0:T(8,128)(2,1)} custom-call(s32[2,6]{1,0:T(2,128)} %lists_ref.3, bf16[12,4,128,128]{3,2,1,0:T(8,128)(2,1)} %get-tuple-element.9.h_ref, f32[12,4,8,128]{3,2,1,0:T(8,128)} %get-tuple-element.10.sq_ref), custom_call_target="tpu_custom_call" | custom-call | flops 4529848320 | bytes 4194304 | tf_op jit(solution)/shard_map/second/pallas_call | solution.py:365
  52.4 0.0 collective-permute-done.next_ref
  52.4 0.0 copy-start
  52.4 0.8 %copy-done = bf16[11,128,128]{2,1,0:T(8,128)(2,1)} copy-done((bf16[11,128,128]{2,1,0:T(8,128)(2,1)}, bf16[11,128,128]{2,1,0:T(8,128)(2,1)S(1)}, u32[]{:S(2)}) %copy-start) | copy-done | bytes 360472
  53.2 4.3 %back.1 = f32[2,13,128,128]{3,2,1,0:T(8,128)} custom-call(bf16[7,10,128,128]{3,2,1,0:T(8,128)(2,1)} %gather.1.g_ref, bf16[11,128,128]{2,1,0:T(8,128)(2,1)} %get-tuple-element.8.band0_ref, bf16[11,128,128]{2,1,0:T(8,128)(2,1)} %second.1.band1_ref, bf16[11,128,128]{2,1,0:T(8,128)(2,1)} %copy-done), custom_call_target="tpu_custom_call" | custom-call | tf_op jit(solution)/shard_map/back/pallas_call | solution.py:375
  (2 shorter events, 0.0 us)
Async XLA Ops:
  38.5 14.0 %collective-permute-start = (bf16[11,128,128]{2,1,0:T(8,128)(2,1)}, bf16[11,128,128]{2,1,0:T(8,128)(2,1)S(1)}, u32[]{:S(2)}, u32[]{:S(2)}) collective-permute-start(bf16[11,128,128]{2,1,0:T(8,128)(2,1)} %get-tuple-element.8.band0_ref), channel_id=1, source_target_pairs={{1,0},{2,1},{3,2},{4,3},{5,4},{6,5},{7,6},{8,7},{9,8},{10,9},{11,1... | collective-permute-start | bytes 1081352 | tf_op jit(solution)/shard_map/ppermute | solution.py:364
  52.4 0.8 %copy-start = (bf16[11,128,128]{2,1,0:T(8,128)(2,1)}, bf16[11,128,128]{2,1,0:T(8,128)(2,1)S(1)}, u32[]{:S(2)}) copy-start(bf16[11,128,128]{2,1,0:T(8,128)(2,1)S(1)} %collective-permute-done.next_ref) | copy-start | bytes 1081348

commit v2 on v1

v2 whole, which is shorter than its diff:
```python
import functools
import math

import jax
import jax.numpy as jnp
from jax import lax
from jax.experimental import pallas as pl
from jax.experimental.pallas import tpu as pltpu
from jax.sharding import PartitionSpec as P

RO = 3
Q = 5
STEPS = 3
CHEM = 0.25
AXES = ("space", "inner")
MESH = pl.DeviceIdType.MESH
BF = jnp.bfloat16
F32 = jnp.float32
PER = 5
REACH = 3
HALF = 5
VMEM_LIMIT = 60 * 1024 * 1024


def exchange_parts(total, inner, g_ref, pay_ref, next_ref, band_ref, send_sem, recv_sem, band_sem):
    me = lax.axis_index("space") * inner + lax.axis_index("inner")
    core = lax.rem(me, 2)
    even = core == 0
    odd = core == 1
    chip_odd = lax.rem(me // 2, 2) == 1
    chip_even = lax.rem(me // 2, 2) == 0
    partner = me + 1 - 2 * core
    across = jnp.where(chip_odd, me - 2, me + 2)
    far = jnp.where(odd, me + 3, me - 3)
    side = jnp.where(odd, me + 1, me - 1)
    has_low = me >= 4
    has_high = me + 4 < total
    has_far = (far >= 0) & (far < total)
    has_side = (side >= 0) & (side < total)

    def place(device):
        return (device // inner, lax.rem(device, inner))

    def greet():
        barrier = pltpu.get_barrier_semaphore()

        def one(device):
            pl.semaphore_signal(barrier, inc=1, device_id=place(device), device_id_type=MESH)

        one(partner)
        one(across)
        pl.when(has_low)(lambda: one(me - 4))
        pl.when(has_high)(lambda: one(me + 4))
        pl.when(has_far)(lambda: one(far))
        pl.when(has_side)(lambda: one(side))

    def meet():
        peers = jnp.int32(2)
        for has in (has_low, has_high, has_far, has_side):
            peers = peers + has.astype(jnp.int32)
        pl.semaphore_wait(pltpu.get_barrier_semaphore(), peers)

    def clear():
        for slot in range(2 * REACH + 1):
            if slot != REACH:
                source = me + slot - REACH

                @pl.when((source < 0) | (source >= total))
                def _():
                    g_ref[slot] = jnp.zeros(g_ref.shape[1:], g_ref.dtype)

        @pl.when(me == total - 1)
        def _():
            next_ref[...] = jnp.zeros(next_ref.shape, next_ref.dtype)

    def copy(src, dst_slot, lo, hi, number, part, device):
        return pltpu.make_async_remote_copy(
            src_ref=src.at[pl.ds(lo, hi - lo)],
            dst_ref=g_ref.at[dst_slot, pl.ds(lo, hi - lo)],
            send_sem=send_sem.at[number, part],
            recv_sem=recv_sem.at[dst_slot, part],
            device_id=place(device),
            device_id_type=MESH,
        )

    whole = ((0, 0, HALF), (1, HALF, 2 * HALF))
    tail = ((0, 2, HALF), (1, HALF, 2 * HALF))
    head = ((0, 0, HALF), (1, HALF, HALF + 2))

    def copies(src, slot, number, device, pieces):
        return [copy(src, slot, lo, hi, number, part, device) for part, lo, hi in pieces]

    up = copies(pay_ref, 1, 0, across, whole)
    down = copies(pay_ref, 5, 0, across, whole)
    far_up = copies(pay_ref, 0, 1, far, tail)
    far_down = copies(pay_ref, 6, 1, far, head)
    side_up = copies(pay_ref, 2, 2, partner, whole)
    side_down = copies(pay_ref, 4, 2, partner, whole)
    relay_up = copies(g_ref.at[5], 1, 3, me + 4, whole)
    relay_down = copies(g_ref.at[1], 5, 3, me - 4, whole)
    low0 = copies(g_ref.at[1], 0, 4, partner, tail)
    low1 = copies(g_ref.at[1], 2, 4, partner, whole)
    high0 = copies(g_ref.at[5], 4, 5, partner, whole)
    high1 = copies(g_ref.at[5], 6, 5, partner, head)
    got_low = chip_odd | has_low
    got_high = chip_even | has_high

    def send():
        for part in range(2):
            pl.when(has_far & odd)(lambda: far_up[part].start())
            pl.when(has_far & even)(lambda: far_down[part].start())
            pl.when(chip_even)(lambda: up[part].start())
            pl.when(chip_odd)(lambda: down[part].start())
            pl.when(even)(lambda: side_up[part].start())
            pl.when(odd)(lambda: side_down[part].start())

    def pass_low(part):
        up[part].wait_recv()
        pl.when(chip_odd & has_low)(lambda: relay_down[part].start())
        pl.when(even)(lambda: low0[part].start())
        pl.when(odd)(lambda: low1[part].start())

    def pass_high(part):
        down[part].wait_recv()
        pl.when(chip_even & has_high)(lambda: relay_up[part].start())
        pl.when(even)(lambda: high0[part].start())
        pl.when(odd)(lambda: high1[part].start())

    def forward():
        for part in range(2):
            pl.when(chip_odd)(lambda: pass_low(part))
            pl.when(chip_even)(lambda: pass_high(part))
        for part in range(2):
            pl.when(chip_even & has_low)(lambda: pass_low(part))
            pl.when(chip_odd & has_high)(lambda: pass_high(part))

    def receive():
        for part in range(2):

            @pl.when(even)
            def _():
                pl.when(has_far)(lambda: far_up[part].wait_recv())
                pl.when(got_low)(lambda: low1[part].wait_recv())
                side_down[part].wait_recv()
                pl.when(got_high)(lambda: high1[part].wait_recv())

            @pl.when(odd)
            def _():
                pl.when(got_low)(lambda: low0[part].wait_recv())
                side_up[part].wait_recv()
                pl.when(got_high)(lambda: high0[part].wait_recv())
                pl.when(has_far)(lambda: far_down[part].wait_recv())

    def drain():
        for part in range(2):

            @pl.when(even)
            def _():
                pl.when(has_far)(lambda: far_down[part].wait_send())
                side_up[part].wait_send()
                pl.when(got_low)(lambda: low0[part].wait_send())
                pl.when(got_high)(lambda: high0[part].wait_send())

            @pl.when(odd)
            def _():
                pl.when(has_far)(lambda: far_up[part].wait_send())
                side_down[part].wait_send()
                pl.when(got_low)(lambda: low1[part].wait_send())
                pl.when(got_high)(lambda: high1[part].wait_send())

            pl.when(chip_even)(lambda: up[part].wait_send())
            pl.when(chip_odd)(lambda: down[part].wait_send())
            pl.when(chip_even & has_high)(lambda: relay_up[part].wait_send())
            pl.when(chip_odd & has_low)(lambda: relay_down[part].wait_send())

    band_copy = pltpu.make_async_remote_copy(
        src_ref=band_ref,
        dst_ref=next_ref,
        send_sem=band_sem.at[0],
        recv_sem=band_sem.at[1],
        device_id=place(me - 1),
        device_id_type=MESH,
    )

    def band_send():
        pl.when(me >= 1)(lambda: band_copy.start())

    def band_wait():
        pl.when(me < total - 1)(lambda: band_copy.wait_recv())
        pl.when(me >= 1)(lambda: band_copy.wait_send())

    return me, greet, meet, clear, send, forward, receive, drain, band_send, band_wait


def prepare(first, pattern_ref, ham_ref, ortho_ref, pay_ref, g_ref):
    bs = ham_ref.shape[-1]
    eye = jnp.where(eye_mask(bs, bs), 1.0, 0.0)
    for c in range(ham_ref.shape[0]):
        blocks = [
            jnp.where(first + c == 0, 0.0, ortho_ref[c, 0].astype(F32)),
            ortho_ref[c, 1].astype(F32) + eye,
        ]
        for r in range(3):
            keep = pattern_ref[c, r + 2].astype(F32)
            blocks.append(ham_ref[c, r + 2].astype(F32) * keep)
        for which, block in enumerate(blocks):
            block = block.astype(BF)
            pay_ref[c * PER + which] = block
            g_ref[REACH, c * PER + which] = block


def main_kernel(
    total,
    inner,
    lists_ref,
    pattern_ref,
    ham_ref,
    ortho_ref,
    g_ref,
    band0_ref,
    band1_ref,
    next_ref,
    pay_ref,
    h_ref,
    sq_ref,
    zt_ref,
    x_ref,
    m_ref,
    y_ref,
    pc_ref,
    send_sem,
    recv_sem,
    band_sem,
):
    me, greet, meet, clear, send, forward, receive, drain, band_send, band_wait = exchange_parts(
        total, inner, g_ref, pay_ref, next_ref, band0_ref, send_sem, recv_sem, band_sem
    )
    first = me * lists_ref.shape[0]
    greet()
    prepare(first, pattern_ref, ham_ref, ortho_ref, pay_ref, g_ref)
    clear()
    meet()
    send()
    forward()
    receive()
    orth_stage(g_ref, h_ref, sq_ref, zt_ref)
    work = (x_ref, m_ref, y_ref, pc_ref)
    assemble(0, lists_ref, first, h_ref, sq_ref, x_ref)
    iterate(0, lists_ref, first, band0_ref, *work)
    assemble(1, lists_ref, first, h_ref, sq_ref, x_ref)
    band_send()
    iterate(1, lists_ref, first, band1_ref, *work)
    drain()
    band_wait()


def block_of(g_ref, column, which):
    index = column + 2 * REACH
    return g_ref[index // 2, (index % 2) * PER + which]


def dot(left, right):
    return jnp.dot(left, right, preferred_element_type=F32)


def eye_mask(rows, columns, shift=0):
    row = lax.broadcasted_iota(jnp.int32, (rows, columns), 0) + shift
    return row == lax.broadcasted_iota(jnp.int32, (rows, columns), 1)


def fold(square):
    n = square.shape[0]
    return jnp.sum(square.reshape(n // 8, 8, square.shape[1]), axis=0)


def orth_stage(g_ref, h_ref, sq_ref, zt_ref):
    bs = g_ref.shape[-1]
    last = Q + 1
    quarter = jnp.where(eye_mask(bs, bs), CHEM, 0.0)
    for a in range(-Q, last + 1):
        zt_ref[a + Q] = jnp.concatenate(
            [block_of(g_ref, a, 0).T, block_of(g_ref, a, 1).T], axis=1
        )
    for b in range(-Q, last + 1):
        count = min(RO + 1, last - b + 1)
        z_col = jnp.concatenate([block_of(g_ref, b, 0), block_of(g_ref, b, 1)], axis=0)
        below = block_of(g_ref, b - 1, 3)
        rows = [jnp.concatenate([block_of(g_ref, b - 1, 2), below.T], axis=1)]
        rows.append(jnp.concatenate([below, block_of(g_ref, b, 2)], axis=1))
        if count >= 2:
            rows.append(jnp.concatenate([block_of(g_ref, b - 1, 4), block_of(g_ref, b, 3)], axis=1))
        product = dot(jnp.concatenate(rows, axis=0), z_col).astype(BF)
        if count >= 3:
            tail = dot(block_of(g_ref, b, 4), z_col[bs:]).astype(BF)
            product = jnp.concatenate([product, tail], axis=0)
        for off in range(count):
            transposed = zt_ref[b + off + Q]
            if off < RO:
                value = dot(transposed, product[off * bs : (off + 2) * bs])
            else:
                value = dot(transposed[:, :bs], product[off * bs : (off + 1) * bs])
            value = value.astype(BF)
            h_ref[b + Q, off] = value
            wide = value.astype(F32)
            if off == 0:
                wide = quarter - wide
            sq_ref[b + Q, off] = fold(wide * wide)


def assemble(which, lists_ref, first, h_ref, sq_ref, x_ref):
    bs = h_ref.shape[-1]
    slot_count = lists_ref.shape[1]
    slots = [lists_ref[which, s] for s in range(slot_count)]
    live = [slot >= 0 for slot in slots]
    place = [jnp.clip(slot - first + Q, 0, 2 * Q + 1) for slot in slots]
    total = jnp.zeros((8, bs), F32)
    live_count = jnp.int32(0)
    pick = {}
    for s in range(slot_count):
        live_count = live_count + live[s].astype(jnp.int32)
        for t in range(s + 1):
            low = jnp.minimum(place[s], place[t])
            off = jnp.maximum(place[s], place[t]) - low
            valid = live[s] & live[t] & (off <= RO)
            off = jnp.minimum(off, RO)
            pick[s, t] = (low, off, valid)
            part = jnp.where(valid, sq_ref[low, off], 0.0)
            total = total + (part if s == t else 2.0 * part)
    total = jnp.sum(jnp.sum(total, axis=1, keepdims=True), axis=0, keepdims=True)
    rows = jnp.full((1, 1), live_count * bs, jnp.int32).astype(F32)
    scale = 2.0 * jnp.sqrt(total / rows + 1e-06)
    inverse = 1.0 / scale
    eye = eye_mask(bs, bs)
    for s in range(slot_count):
        for t in range(s + 1):
            low, off, valid = pick[s, t]
            value = h_ref[low, off].astype(F32)
            if s == t:
                value = jnp.where(eye, CHEM, 0.0) - value
            else:
                value = -value
            value = jnp.where(valid, value * inverse, 0.0)
            here, there = pl.ds(s * bs, bs), pl.ds(t * bs, bs)
            if s == t:
                x_ref[here, here] = value.astype(BF)
            else:
                flipped = value.T
                straight = place[s] >= place[t]
                x_ref[here, there] = jnp.where(straight, value, flipped).astype(BF)
                x_ref[there, here] = jnp.where(straight, flipped, value).astype(BF)


def iterate(which, lists_ref, first, band_ref, x_ref, m_ref, y_ref, pc_ref):
    bs = pc_ref.shape[-1]
    slot_count = lists_ref.shape[1]
    order = slot_count * bs
    chunk = math.gcd(order, 256)
    source, target = x_ref, y_ref
    for step in range(STEPS - 1):
        for at in range(0, order, chunk):
            square = dot(source[pl.ds(at, chunk), :], source[...])
            unit = jnp.where(eye_mask(chunk, order, at), 1.5, 0.0)
            m_ref[pl.ds(at, chunk), :] = (unit - 0.5 * square).astype(BF)
        for at in range(0, order, chunk):
            target[pl.ds(at, chunk), :] = dot(source[pl.ds(at, chunk), :], m_ref[...]).astype(BF)
        source, target = target, source
    columns = source[:, :bs]
    for at in range(0, order, chunk):
        square = dot(source[pl.ds(at, chunk), :], columns)
        unit = jnp.where(eye_mask(chunk, bs, at), 1.5, 0.0)
        m_ref[pl.ds(at, chunk), :bs] = (unit - 0.5 * square).astype(BF)
    factor = m_ref[:, :bs]
    for s in range(slot_count):
        result = dot(source[pl.ds(s * bs, bs), :], factor)
        if s == 0:
            result = result + jnp.where(eye_mask(bs, bs), 1.0, 0.0)
        pc_ref[s] = (0.5 * result).astype(BF)
    for r in range(2 * Q + 1):
        at = jnp.int32(0)
        found = jnp.bool_(False)
        for s in range(slot_count):
            slot = lists_ref[which, s]
            hit = (slot >= 0) & (slot == first + which + r - Q)
            at = jnp.where(hit, s, at)
            found = found | hit
        band_ref[r] = jnp.where(found, pc_ref[at], jnp.zeros((bs, bs), BF))


def back_kernel(g_ref, band0_ref, band1_ref, next_ref, out_ref):
    bs = g_ref.shape[-1]
    zero = jnp.zeros((bs, bs), BF)
    for column in range(2):
        mine = (band0_ref, band1_ref)[column]
        after = (band1_ref, next_ref)[column]
        right = jnp.concatenate(
            [block_of(g_ref, column, 1).T, block_of(g_ref, column + 1, 0).T], axis=0
        )
        rows = []
        for i in range(2 * Q + 2):
            here = mine[i] if i <= 2 * Q else zero
            there = after[i - 1] if i >= 1 else zero
            rows.append(jnp.concatenate([here, there], axis=1))
        y = dot(jnp.concatenate(rows, axis=0), right).astype(BF)
        for p in range(2 * Q + 3):
            a = column + p - Q - 1
            if p == 0:
                value = dot(block_of(g_ref, a + 1, 0), y[:bs])
            elif p == 2 * Q + 2:
                value = dot(block_of(g_ref, a, 1), y[(p - 1) * bs : p * bs])
            else:
                left = jnp.concatenate(
                    [block_of(g_ref, a, 1), block_of(g_ref, a + 1, 0)], axis=1
                )
                value = dot(left, y[(p - 1) * bs : (p + 1) * bs])
            out_ref[column, p] = value


def vmem():
    return pl.BlockSpec(memory_space=pltpu.VMEM)


def smem():
    return pl.BlockSpec(memory_space=pltpu.SMEM)


def local(total, inner, hamiltonian, pattern, ortho, lists):
    local_count, _, bs = hamiltonian.shape[:3]
    slot_count = lists.shape[1]
    order = slot_count * bs
    params = pltpu.CompilerParams(vmem_limit_bytes=VMEM_LIMIT)
    band_shape = jax.ShapeDtypeStruct((2 * Q + 1, bs, bs), BF)
    orth_cols = 2 * Q + local_count
    payload = (local_count * PER, bs, bs)
    gathered, band0, band1, following = pl.pallas_call(
        functools.partial(main_kernel, total, inner),
        out_shape=(
            jax.ShapeDtypeStruct((2 * REACH + 1,) + payload, BF),
            band_shape,
            band_shape,
            band_shape,
        ),
        in_specs=[smem(), smem(), vmem(), vmem()],
        out_specs=(vmem(),) * 4,
        scratch_shapes=[
            pltpu.VMEM(payload, BF),
            pltpu.VMEM((orth_cols, RO + 1, bs, bs), BF),
            pltpu.VMEM((orth_cols, RO + 1, 8, bs), F32),
            pltpu.VMEM((orth_cols, bs, 2 * bs), BF),
            pltpu.VMEM((order, order), BF),
            pltpu.VMEM((order, order), BF),
            pltpu.VMEM((order, order), BF),
            pltpu.VMEM((slot_count, bs, bs), BF),
            pltpu.SemaphoreType.DMA((6, 2)),
            pltpu.SemaphoreType.DMA((2 * REACH + 1, 2)),
            pltpu.SemaphoreType.DMA((2,)),
        ],
        compiler_params=pltpu.CompilerParams(
            collective_id=0, has_side_effects=True, vmem_limit_bytes=VMEM_LIMIT
        ),
        name="main",
    )(lists, pattern, hamiltonian, ortho)
    return pl.pallas_call(
        back_kernel,
        out_shape=jax.ShapeDtypeStruct((local_count, 2 * Q + 3, bs, bs), F32),
        in_specs=[vmem()] * 4,
        out_specs=vmem(),
        compiler_params=params,
        name="back",
    )(gathered, band0, band1, following)


def solution(mesh):
    in_specs = (
        P(AXES, None, None, None),
        P(AXES, None),
        P(AXES, None, None, None),
        P(AXES, None),
    )
    inner = mesh.shape["inner"]
    total = mesh.shape["space"] * inner
    return jax.shard_map(
        functools.partial(local, total, inner),
        mesh=mesh,
        in_specs=in_specs,
        out_specs=P(AXES, None, None, None),
        check_vma=False,
    )
```

time: 57.8 us -> 41.1 us (0.71)
  the two profiles are of different devices: /device:TPU:4 before, /device:TPU:1 now
where the time goes in v2:
time: 41.1 us; the launch traced here: 40.9 us
  Pallas kernels  40.9 us (100%)
    pallas_call x1, Pallas kernels, local(): pl.pallas_call(functools.partial(main_kernel, total, inner), out_shape=(j...  36.7 us
    pallas_call x1, Pallas kernels, local(): pl.pallas_call(back_kernel, out_shape=jax.ShapeDtypeStruct((local_count,...  4.28 us

profile of v2, /device:TPU:1, one launch (start us, length us, event | category | flops | bytes accessed | tf_op | source)
XLA Modules:
  0.0 40.9 jit_solution(7920789824863388024)
XLA Ops:
  0.0 36.7 %main.1 = (bf16[7,10,128,128]{3,2,1,0:T(8,128)(2,1)}, bf16[11,128,128]{2,1,0:T(8,128)(2,1)}, bf16[11,128,128]{2,1,0:T(8,128)(2,1)}, bf16[11,128,128]{2,1,0:T(8,128)(2,1)}) custom-call(s32[2,6]{1,0:T(2,128)} %lists_ref.1, s32[2,5]{1,0:T(2,128)} %pattern_ref.1, bf16[2,5,128,128]{3,2,1,0:T(8,128)(2,1)} %ham_ref.1, bf16[2,2,128,128]{3,2,1,0:T(8,128)(2,1)} %ortho_ref.1), custom_call_target="tpu_custom_call" | custom-call | tf_op jit(solution)/shard_map/main/pallas_call | solution.py:434
  36.7 4.3 %back.1 = f32[2,13,128,128]{3,2,1,0:T(8,128)} custom-call(bf16[7,10,128,128]{3,2,1,0:T(8,128)(2,1)} %get-tuple-element.9.g_ref, bf16[11,128,128]{2,1,0:T(8,128)(2,1)} %get-tuple-element.10.band0_ref, bf16[11,128,128]{2,1,0:T(8,128)(2,1)} %get-tuple-element.11.band1_ref, bf16[11,128,128]{2,1,0:T(8,128)(2,1)} %get-tuple-element.12.next_ref), custom_call_target="tpu_custom_call" | custom-call | tf_op jit(solution)/shard_map/back/pallas_call | solution.py:462

commit v3 on v2

--- a/solution.py
+++ b/solution.py
@@ -216,10 +216,11 @@
     pattern_ref,
     ham_ref,
     ortho_ref,
-    g_ref,
+    z_ref,
     band0_ref,
     band1_ref,
     next_ref,
+    g_ref,
     pay_ref,
     h_ref,
     sq_ref,
@@ -231,6 +232,7 @@
     send_sem,
     recv_sem,
     band_sem,
+    z_sem,
 ):
     me, greet, meet, clear, send, forward, receive, drain, band_send, band_wait = exchange_parts(
         total, inner, g_ref, pay_ref, next_ref, band0_ref, send_sem, recv_sem, band_sem
@@ -243,6 +245,11 @@
     send()
     forward()
     receive()
+    z_copies = []
+    for column in range(1, z_ref.shape[0]):
+        block = g_ref.at[column // 2, pl.ds((column % 2) * PER, 2)]
+        z_copies.append(pltpu.make_async_copy(block, z_ref.at[column], z_sem.at[column]))
+        z_copies[-1].start()
     orth_stage(g_ref, h_ref, sq_ref, zt_ref)
     work = (x_ref, m_ref, y_ref, pc_ref)
     assemble(0, lists_ref, first, h_ref, sq_ref, x_ref)
@@ -251,6 +258,8 @@
     band_send()
     iterate(1, lists_ref, first, band1_ref, *work)
     drain()
+    for z_copy in z_copies:
+        z_copy.wait()
     band_wait()
 
 
@@ -356,13 +365,22 @@
     order = slot_count * bs
     chunk = math.gcd(order, 256)
     source, target = x_ref, y_ref
+
+    def mirrored(out_ref, at, value):
+        width = value.shape[1]
+        out_ref[pl.ds(at, chunk), :width] = value.astype(BF)
+        for left in range(0, at, chunk):
+            flipped = value[:, left : left + chunk].T
+            out_ref[pl.ds(left, chunk), pl.ds(at, chunk)] = flipped.astype(BF)
+
     for step in range(STEPS - 1):
         for at in range(0, order, chunk):
-            square = dot(source[pl.ds(at, chunk), :], source[...])
-            unit = jnp.where(eye_mask(chunk, order, at), 1.5, 0.0)
-            m_ref[pl.ds(at, chunk), :] = (unit - 0.5 * square).astype(BF)
+            width = at + chunk
+            square = dot(source[pl.ds(at, chunk), :], source[:, :width])
+            unit = jnp.where(eye_mask(chunk, width, at), 1.5, 0.0)
+            mirrored(m_ref, at, unit - 0.5 * square)
         for at in range(0, order, chunk):
-            target[pl.ds(at, chunk), :] = dot(source[pl.ds(at, chunk), :], m_ref[...]).astype(BF)
+            mirrored(target, at, dot(source[pl.ds(at, chunk), :], m_ref[:, : at + chunk]))
         source, target = target, source
     columns = source[:, :bs]
     for at in range(0, order, chunk):
@@ -386,14 +404,19 @@
         band_ref[r] = jnp.where(found, pc_ref[at], jnp.zeros((bs, bs), BF))
 
 
-def back_kernel(g_ref, band0_ref, band1_ref, next_ref, out_ref):
-    bs = g_ref.shape[-1]
+def back_kernel(z_ref, band0_ref, band1_ref, next_ref, result_ref, out_ref, out_sem):
+    bs = z_ref.shape[-1]
     zero = jnp.zeros((bs, bs), BF)
+
+    def z_of(column, which):
+        return z_ref[column + 2 * REACH, which]
+
+    sends = []
     for column in range(2):
         mine = (band0_ref, band1_ref)[column]
         after = (band1_ref, next_ref)[column]
         right = jnp.concatenate(
-            [block_of(g_ref, column, 1).T, block_of(g_ref, column + 1, 0).T], axis=0
+            [z_of(column, 1).T, z_of(column + 1, 0).T], axis=0
         )
         rows = []
         for i in range(2 * Q + 2):
@@ -404,15 +427,26 @@
         for p in range(2 * Q + 3):
             a = column + p - Q - 1
             if p == 0:
-                value = dot(block_of(g_ref, a + 1, 0), y[:bs])
+                value = dot(z_of(a + 1, 0), y[:bs])
             elif p == 2 * Q + 2:
-                value = dot(block_of(g_ref, a, 1), y[(p - 1) * bs : p * bs])
+                value = dot(z_of(a, 1), y[(p - 1) * bs : p * bs])
             else:
                 left = jnp.concatenate(
-                    [block_of(g_ref, a, 1), block_of(g_ref, a + 1, 0)], axis=1
+                    [z_of(a, 1), z_of(a + 1, 0)], axis=1
                 )
                 value = dot(left, y[(p - 1) * bs : (p + 1) * bs])
             out_ref[column, p] = value
+            if p in (Q, 2 * Q + 2):
+                part = pl.ds(0, Q + 1) if p == Q else pl.ds(Q + 1, Q + 2)
+                send = pltpu.make_async_copy(
+                    out_ref.at[column, part],
+                    result_ref.at[column, part],
+                    out_sem.at[column, len(sends) % 2],
+                )
+                send.start()
+                sends.append(send)
+    for send in sends:
+        send.wait()
 
 
 def vmem():
@@ -431,10 +465,10 @@
     band_shape = jax.ShapeDtypeStruct((2 * Q + 1, bs, bs), BF)
     orth_cols = 2 * Q + local_count
     payload = (local_count * PER, bs, bs)
-    gathered, band0, band1, following = pl.pallas_call(
+    z_blocks, band0, band1, following = pl.pallas_call(
         functools.partial(main_kernel, total, inner),
         out_shape=(
-            jax.ShapeDtypeStruct((2 * REACH + 1,) + payload, BF),
+            jax.ShapeDtypeStruct(((2 * REACH + 1) * local_count, 2, bs, bs), BF),
             band_shape,
             band_shape,
             band_shape,
@@ -442,6 +476,7 @@
         in_specs=[smem(), smem(), vmem(), vmem()],
         out_specs=(vmem(),) * 4,
         scratch_shapes=[
+            pltpu.VMEM((2 * REACH + 1,) + payload, BF),
             pltpu.VMEM(payload, BF),
             pltpu.VMEM((orth_cols, RO + 1, bs, bs), BF),
             pltpu.VMEM((orth_cols, RO + 1, 8, bs), F32),
@@ -453,6 +488,7 @@
             pltpu.SemaphoreType.DMA((6, 2)),
             pltpu.SemaphoreType.DMA((2 * REACH + 1, 2)),
             pltpu.SemaphoreType.DMA((2,)),
+            pltpu.SemaphoreType.DMA(((2 * REACH + 1) * local_count,)),
         ],
         compiler_params=pltpu.CompilerParams(
             collective_id=0, has_side_effects=True, vmem_limit_bytes=VMEM_LIMIT
@@ -463,10 +499,14 @@
         back_kernel,
         out_shape=jax.ShapeDtypeStruct((local_count, 2 * Q + 3, bs, bs), F32),
         in_specs=[vmem()] * 4,
-        out_specs=vmem(),
+        out_specs=pl.BlockSpec(memory_space=pl.ANY),
+        scratch_shapes=[
+            pltpu.VMEM((local_count, 2 * Q + 3, bs, bs), F32),
+            pltpu.SemaphoreType.DMA((local_count, 2)),
+        ],
         compiler_params=params,
         name="back",
-    )(gathered, band0, band1, following)
+    )(z_blocks, band0, band1, following)
 
 
 def solution(mesh):

time: 41.1 us -> 39.8 us (0.968)
  Pallas kernels: 40.9 us -> 39.7 us
    pallas_call x1, Pallas kernels: 4.28 us -> 3.48 us  [local(): pl.pallas_call(back_kernel, out_shape=jax.ShapeDtypeStruct((local_count,...]
    pallas_call x1, Pallas kernels: 36.7 us -> 36.2 us  [local(): pl.pallas_call(functools.partial(main_kernel, total, inner), out_shape=(j...]
where the time goes in v3:
time: 39.8 us; the launch traced here: 39.7 us
  Pallas kernels  39.7 us (100%)
    pallas_call x1, Pallas kernels, local(): pl.pallas_call(functools.partial(main_kernel, total, inner), out_shape=(j...  36.2 us
    pallas_call x1, Pallas kernels, local(): pl.pallas_call(back_kernel, out_shape=jax.ShapeDtypeStruct((local_count,...  3.48 us

profile of v3, /device:TPU:1, one launch (start us, length us, event | category | flops | bytes accessed | tf_op | source)
XLA Modules:
  0.0 39.7 jit_solution(10264661082441297964)
XLA Ops:
  0.0 36.2 %main.1 = (bf16[14,2,128,128]{3,2,1,0:T(8,128)(2,1)}, bf16[11,128,128]{2,1,0:T(8,128)(2,1)}, bf16[11,128,128]{2,1,0:T(8,128)(2,1)}, bf16[11,128,128]{2,1,0:T(8,128)(2,1)}) custom-call(s32[2,6]{1,0:T(2,128)} %lists_ref.1, s32[2,5]{1,0:T(2,128)} %pattern_ref.1, bf16[2,5,128,128]{3,2,1,0:T(8,128)(2,1)} %ham_ref.1, bf16[2,2,128,128]{3,2,1,0:T(8,128)(2,1)} %ortho_ref.1), custom_call_target="tpu_custom_call" | custom-call | tf_op jit(solution)/shard_map/main/pallas_call | solution.py:468
  36.2 3.5 %back.1 = f32[2,13,128,128]{3,2,1,0:T(8,128)} custom-call(bf16[14,2,128,128]{3,2,1,0:T(8,128)(2,1)} %get-tuple-element.9.z_ref, bf16[11,128,128]{2,1,0:T(8,128)(2,1)} %get-tuple-element.10.band0_ref, bf16[11,128,128]{2,1,0:T(8,128)(2,1)} %get-tuple-element.11.band1_ref, bf16[11,128,128]{2,1,0:T(8,128)(2,1)} %get-tuple-element.12.next_ref), custom_call_target="tpu_custom_call" | custom-call | tf_op jit(solution)/shard_map/back/pallas_call | solution.py:498

commit v4 on v3

--- a/solution.py
+++ b/solution.py
@@ -126,30 +126,54 @@
         pl.when(even)(lambda: high0[part].start())
         pl.when(odd)(lambda: high1[part].start())
 
-    def forward():
-        for part in range(2):
-            pl.when(chip_odd)(lambda: pass_low(part))
-            pl.when(chip_even)(lambda: pass_high(part))
-        for part in range(2):
-            pl.when(chip_even & has_low)(lambda: pass_low(part))
-            pl.when(chip_odd & has_high)(lambda: pass_high(part))
-
-    def receive():
+    def receive_low():
         for part in range(2):
 
             @pl.when(even)
             def _():
                 pl.when(has_far)(lambda: far_up[part].wait_recv())
                 pl.when(got_low)(lambda: low1[part].wait_recv())
-                side_down[part].wait_recv()
-                pl.when(got_high)(lambda: high1[part].wait_recv())
 
             @pl.when(odd)
             def _():
                 pl.when(got_low)(lambda: low0[part].wait_recv())
                 side_up[part].wait_recv()
+
+    def receive_high():
+        for part in range(2):
+
+            @pl.when(even)
+            def _():
+                side_down[part].wait_recv()
+                pl.when(got_high)(lambda: high1[part].wait_recv())
+
+            @pl.when(odd)
+            def _():
                 pl.when(got_high)(lambda: high0[part].wait_recv())
                 pl.when(has_far)(lambda: far_down[part].wait_recv())
+
+    def receive(orth):
+        @pl.when(chip_odd)
+        def _():
+            for part in range(2):
+                pass_low(part)
+            receive_low()
+            orth(range(-Q, 2), range(-Q, -1))
+            for part in range(2):
+                pl.when(has_high)(lambda: pass_high(part))
+            receive_high()
+            orth(range(2, Q + 2), range(-1, Q + 2))
+
+        @pl.when(chip_even)
+        def _():
+            for part in range(2):
+                pass_high(part)
+            receive_high()
+            orth(range(0, Q + 2), range(1, Q + 2))
+            for part in range(2):
+                pl.when(has_low)(lambda: pass_low(part))
+            receive_low()
+            orth(range(-Q, 0), range(-Q, 1))
 
     def drain():
         for part in range(2):
@@ -189,7 +213,7 @@
         pl.when(me < total - 1)(lambda: band_copy.wait_recv())
         pl.when(me >= 1)(lambda: band_copy.wait_send())
 
-    return me, greet, meet, clear, send, forward, receive, drain, band_send, band_wait
+    return me, greet, meet, clear, send, receive, drain, band_send, band_wait
 
 
 def prepare(first, pattern_ref, ham_ref, ortho_ref, pay_ref, g_ref):
@@ -234,7 +258,7 @@
     band_sem,
     z_sem,
 ):
-    me, greet, meet, clear, send, forward, receive, drain, band_send, band_wait = exchange_parts(
+    me, greet, meet, clear, send, receive, drain, band_send, band_wait = exchange_parts(
         total, inner, g_ref, pay_ref, next_ref, band0_ref, send_sem, recv_sem, band_sem
     )
     first = me * lists_ref.shape[0]
@@ -243,19 +267,17 @@
     clear()
     meet()
     send()
-    forward()
-    receive()
+    receive(functools.partial(orth_stage, g_ref, h_ref, sq_ref, zt_ref))
     z_copies = []
     for column in range(1, z_ref.shape[0]):
         block = g_ref.at[column // 2, pl.ds((column % 2) * PER, 2)]
         z_copies.append(pltpu.make_async_copy(block, z_ref.at[column], z_sem.at[column]))
         z_copies[-1].start()
-    orth_stage(g_ref, h_ref, sq_ref, zt_ref)
     work = (x_ref, m_ref, y_ref, pc_ref)
     assemble(0, lists_ref, first, h_ref, sq_ref, x_ref)
     iterate(0, lists_ref, first, band0_ref, *work)
+    band_send()
     assemble(1, lists_ref, first, h_ref, sq_ref, x_ref)
-    band_send()
     iterate(1, lists_ref, first, band1_ref, *work)
     drain()
     for z_copy in z_copies:
@@ -282,15 +304,15 @@
     return jnp.sum(square.reshape(n // 8, 8, square.shape[1]), axis=0)
 
 
-def orth_stage(g_ref, h_ref, sq_ref, zt_ref):
+def orth_stage(g_ref, h_ref, sq_ref, zt_ref, rows_here, columns_here):
     bs = g_ref.shape[-1]
     last = Q + 1
     quarter = jnp.where(eye_mask(bs, bs), CHEM, 0.0)
-    for a in range(-Q, last + 1):
+    for a in rows_here:
         zt_ref[a + Q] = jnp.concatenate(
             [block_of(g_ref, a, 0).T, block_of(g_ref, a, 1).T], axis=1
         )
-    for b in range(-Q, last + 1):
+    for b in columns_here:
         count = min(RO + 1, last - b + 1)
         z_col = jnp.concatenate([block_of(g_ref, b, 0), block_of(g_ref, b, 1)], axis=0)
         below = block_of(g_ref, b - 1, 3)

time: 39.8 us -> 38.9 us (0.977)
  Pallas kernels: 39.7 us -> 38.6 us
    pallas_call x1, Pallas kernels: 36.2 us -> 35.1 us  [local(): pl.pallas_call(functools.partial(main_kernel, total, inner), out_shape=(j...]
where the time goes in v4:
time: 38.9 us; the launch traced here: 38.8 us
  Pallas kernels  38.6 us (99%)
    pallas_call x1, Pallas kernels, local(): pl.pallas_call(functools.partial(main_kernel, total, inner), out_shape=(j...  35.1 us
    pallas_call x1, Pallas kernels, local(): pl.pallas_call(back_kernel, out_shape=jax.ShapeDtypeStruct((local_count,...  3.48 us

profile of v4, /device:TPU:1, one launch (start us, length us, event | category | flops | bytes accessed | tf_op | source)
XLA Modules:
  0.0 38.8 jit_solution(17592400343601719073)
XLA Ops:
  0.0 35.1 %main.1 = (bf16[14,2,128,128]{3,2,1,0:T(8,128)(2,1)}, bf16[11,128,128]{2,1,0:T(8,128)(2,1)}, bf16[11,128,128]{2,1,0:T(8,128)(2,1)}, bf16[11,128,128]{2,1,0:T(8,128)(2,1)}) custom-call(s32[2,6]{1,0:T(2,128)} %lists_ref.1, s32[2,5]{1,0:T(2,128)} %pattern_ref.1, bf16[2,5,128,128]{3,2,1,0:T(8,128)(2,1)} %ham_ref.1, bf16[2,2,128,128]{3,2,1,0:T(8,128)(2,1)} %ortho_ref.1), custom_call_target="tpu_custom_call" | custom-call | tf_op jit(solution)/shard_map/main/pallas_call | solution.py:490
  35.1 3.5 %back.1 = f32[2,13,128,128]{3,2,1,0:T(8,128)} custom-call(bf16[14,2,128,128]{3,2,1,0:T(8,128)(2,1)} %get-tuple-element.9.z_ref, bf16[11,128,128]{2,1,0:T(8,128)(2,1)} %get-tuple-element.10.band0_ref, bf16[11,128,128]{2,1,0:T(8,128)(2,1)} %get-tuple-element.11.band1_ref, bf16[11,128,128]{2,1,0:T(8,128)(2,1)} %get-tuple-element.12.next_ref), custom_call_target="tpu_custom_call" | custom-call | tf_op jit(solution)/shard_map/back/pallas_call | solution.py:520
